TPU v7x, 128 devices: a whole 4x4x4 slice. The times are simulated.
128 devices in a mesh: nodes: 128 (over z, y, x, core).
Axes of the slice: x: 4, y: 4, z: 4, core: 2. Of those that a mesh axis runs over, the one named last changes fastest.
Arguments:
- features: float32 [131072, 768], P('nodes'), may hold values from -6 to 6
- history: float32 [131072, 256], P('nodes'), may hold values from -6 to 6
- request_ids: int32 [128, 128, 16], P('nodes'), may hold values from 0 to 1023
- request_count: int32 [128, 128], P('nodes'), may hold values from 1 to 16, as said below
- halo_ids: int32 [128, 128, 8], P('nodes'), may hold values from 0 to 1023
- halo_count: int32 [128, 128], P('nodes'), may hold values from 1 to 8, as said below
- tile_values: bfloat16 [65536, 128, 128], P('nodes'), may hold values from -0.25 to 0.25
- tile_rows: int32 [65536], P('nodes'), may hold values from 0 to 15
- tile_cols: int32 [65536], P('nodes'), may hold values from 0 to 23
- tile_count: int32 [128], P('nodes'), may hold values from 1 to 512, as said below
- w_in: bfloat16 [768, 256], replicated, may hold values from -0.21875 to 0.21875
- w_out: bfloat16 [256, 256], replicated, may hold values from -0.375 to 0.375
Outputs:
- updated: bfloat16 [262144, 256], P('nodes')
Inputs may be any that keep to these rules, and one draw needn't show every extreme that they name: `request_ids`: slots at or beyond the count are ignored. `request_count`: every cluster fills all 16 slots for some owner, and some owner receives full lists from every cluster. `halo_ids`: slots at or beyond the count are ignored. `halo_count`: every cluster fills all 8 slots for some owner, and some owner receives full lists from every cluster. `tile_count`: some cluster uses all 512 tile slots.
All inputs are finite; a program needn't handle non-finite values.
Results may differ from a plain program's by a relative error of at most 0.0059.
Values may be sent and summed in bfloat16 or wider, within the bound.
No kernel may reach another device: no remote copies, remote signals or barrier semaphores. Data moves between devices by JAX's collectives and lax.ppermute only.
A program may use at most 128 MiB of HBM per device.

v0:
```python
import jax
import jax.numpy as jnp
from jax import lax
from jax.sharding import PartitionSpec as P

GROUP = 64


def aggregate(source, tile_block, row_list, col_list, used, cluster_rows):
    tile_side = tile_block.shape[1]
    hidden = source.shape[1]
    group_size = GROUP
    row_blocks = cluster_rows // tile_side
    blocks = source.reshape(-1, tile_side, hidden)

    def add_group(running, group_index):
        start = group_index * group_size
        vals_group = lax.dynamic_slice_in_dim(tile_block, start, group_size, 0)
        rows_group = lax.dynamic_slice_in_dim(row_list, start, group_size, 0)
        cols_group = lax.dynamic_slice_in_dim(col_list, start, group_size, 0)
        picked = blocks[cols_group]
        products = jnp.einsum(
            "gij,gjk->gik", vals_group, picked, preferred_element_type=jnp.float32
        )
        order = start + jnp.arange(group_size, dtype=jnp.int32)
        live_tiles = (order < used).astype(jnp.float32)
        running = running.at[rows_group].add(products * live_tiles[:, None, None])
        return (running, None)

    start_sum = jnp.zeros((row_blocks, tile_side, hidden), jnp.float32)
    total, _ = lax.scan(
        add_group, start_sum, jnp.arange(tile_block.shape[0] // group_size, dtype=jnp.int32)
    )
    return total.reshape(cluster_rows, hidden)


def on_device(
    features,
    history,
    request_ids,
    request_count,
    halo_ids,
    halo_count,
    tile_values,
    tile_rows,
    tile_cols,
    tile_count,
    w_in,
    w_out,
):
    node_count = lax.axis_size("nodes")
    wanted = request_ids.reshape(node_count, -1)
    wanted_count = request_count.reshape(node_count, 1)
    halo_wanted = halo_ids.reshape(node_count, -1)
    halo_wanted_count = halo_count.reshape(node_count, 1)
    asked, asked_count = (
        lax.all_to_all(wanted, "nodes", split_axis=0, concat_axis=0, tiled=True),
        lax.all_to_all(wanted_count, "nodes", split_axis=0, concat_axis=0, tiled=True),
    )
    halo_asked, halo_asked_count = (
        lax.all_to_all(halo_wanted, "nodes", split_axis=0, concat_axis=0, tiled=True),
        lax.all_to_all(halo_wanted_count, "nodes", split_axis=0, concat_axis=0, tiled=True),
    )
    hidden = w_in.shape[1]
    slot_count = asked.shape[1]
    halo_slots = halo_asked.shape[1]
    width_in = features.shape[1]
    is_live = (jnp.arange(slot_count, dtype=jnp.int32)[None, :] < asked_count).reshape(-1, 1)
    picked_flat = jnp.where(is_live, features[asked.reshape(-1)], 0.0).astype(jnp.bfloat16)
    picked_rows = picked_flat.reshape(node_count, slot_count, width_in)
    halo_live = (jnp.arange(halo_slots, dtype=jnp.int32)[None, :] < halo_asked_count).reshape(-1, 1)
    halo_flat = jnp.where(halo_live, history[halo_asked.reshape(-1)], 0.0).astype(jnp.bfloat16)
    halo_out = halo_flat.reshape(node_count, halo_slots, hidden)
    halo_back = lax.all_to_all(halo_out, "nodes", split_axis=0, concat_axis=0, tiled=True)
    arrived = jnp.einsum(
        "nsd,dh->nsh",
        lax.all_to_all(picked_rows, "nodes", split_axis=0, concat_axis=0, tiled=True),
        w_in,
        preferred_element_type=jnp.float32,
    ).astype(jnp.bfloat16)
    projected = arrived.reshape(-1, hidden)
    halo_block = halo_back.reshape(-1, hidden)
    source = jnp.concatenate([projected, halo_block], axis=0)
    aggregated = aggregate(
        source, tile_values, tile_rows, tile_cols, tile_count[0], projected.shape[0]
    ).astype(jnp.bfloat16)
    mixed = jnp.dot(aggregated, w_out, preferred_element_type=jnp.float32) + projected.astype(
        jnp.float32
    )
    return jax.nn.relu(mixed).astype(jnp.bfloat16)


def solution(mesh):
    in_specs = (
        P("nodes", None),
        P("nodes", None),
        P("nodes", None, None),
        P("nodes", None),
        P("nodes", None, None),
        P("nodes", None),
        P("nodes", None, None),
        P("nodes"),
        P("nodes"),
        P("nodes"),
        P(),
        P(),
    )
    out_specs = P("nodes", None)
    return jax.shard_map(
        on_device, mesh=mesh, in_specs=in_specs, out_specs=out_specs, check_vma=False
    )
```

profile of v0, /device:TPU:1, one launch (start us, length us, event | category | flops | bytes accessed | tf_op | source)
XLA Modules:
  0.0 409.0 jit_solution(2790693744272338573)
XLA Ops:
  0.0 1.5 copy.23
  1.5 11.5 %all-to-all-start = ((s32[128,1,1]{2,1,0:T(1,128)}), s32[128,1,1]{2,1,0:T(1,128)S(1)}, u32[]{:S(2)}, u32[]{:S(2)}) async-start(s32[128,1,1]{2,1,0:T(1,128)} %copy.23), calls=%async_computation | async-start | bytes 131072 | tf_op jit(solution)/shard_map/all_to_all | solution.py:58
  17.3 5.4 %all-to-all-done = s32[128,1,1]{2,1,0:T(1,128)S(1)} async-done(((s32[128,1,1]{2,1,0:T(1,128)}), s32[128,1,1]{2,1,0:T(1,128)S(1)}, u32[]{:S(2)}, u32[]{:S(2)}) %all-to-all-start) | async-done | bytes 544 | tf_op jit(solution)/shard_map/all_to_all | solution.py:58
  22.7 4.5 %all-to-all-start.1 = ((s32[128,1,16]{2,1,0:T(1,128)}), s32[128,1,16]{2,1,0:T(1,128)S(1)}, u32[]{:S(2)}, u32[]{:S(2)}) async-start(s32[128,1,16]{2,1,0:T(1,128)} %bitcast.2), calls=%async_computation.1 | async-start | bytes 131072 | tf_op jit(solution)/shard_map/all_to_all | solution.py:57
  27.2 2.4 reduce
  29.6 7.2 %all-to-all-done.1 = s32[128,1,16]{2,1,0:T(1,128)S(1)} async-done(((s32[128,1,16]{2,1,0:T(1,128)}), s32[128,1,16]{2,1,0:T(1,128)S(1)}, u32[]{:S(2)}, u32[]{:S(2)}) %all-to-all-start.1) | async-done | bytes 8224 | tf_op jit(solution)/shard_map/all_to_all | solution.py:57
  36.8 4.5 %all-to-all-start.3 = ((s32[128,1,1]{2,1,0:T(1,128)}), s32[128,1,1]{2,1,0:T(1,128)S(1)}, u32[]{:S(2)}, u32[]{:S(2)}) async-start(s32[128,1,1]{2,1,0:T(1,128)} %copy.27), calls=%async_computation.3 | async-start | bytes 131072 | tf_op jit(solution)/shard_map/all_to_all | solution.py:62
  42.7 9.1 %gather_fusion.1 = bf16[2048,768]{1,0:T(8,128)(2,1)} fusion(f32[1024,768]{1,0:T(8,128)S(1)} %copy-done, s32[2048]{0:T(1024)S(1)} %broadcast_clamp_fusion), kind=kCustom, calls=%fused_computation.1 | custom fusion | bytes 6299648 | tf_op jit(solution)/shard_map/gather | solution.py:69
  51.8 9.8 %all-to-all-start.4 = ((s32[128,1,8]{2,1,0:T(1,128)}), s32[128,1,8]{2,1,0:T(1,128)S(1)}, u32[]{:S(2)}, u32[]{:S(2)}) async-start(s32[128,1,8]{2,1,0:T(1,128)} %bitcast.8), calls=%async_computation.4 | async-start | bytes 131072 | tf_op jit(solution)/shard_map/all_to_all | solution.py:61
  61.6 3.4 select_convert_fusion
  65.0 6.1 %all-to-all-done.4 = s32[128,1,8]{2,1,0:T(1,128)S(1)} async-done(((s32[128,1,8]{2,1,0:T(1,128)}), s32[128,1,8]{2,1,0:T(1,128)S(1)}, u32[]{:S(2)}, u32[]{:S(2)}) %all-to-all-start.4) | async-done | bytes 4128 | tf_op jit(solution)/shard_map/all_to_all | solution.py:61
  71.1 5.2 %all-to-all-start.2 = ((bf16[128,16,768]{2,1,0:T(8,128)(2,1)}), bf16[128,16,768]{2,1,0:T(8,128)(2,1)}, u32[]{:S(2)}, u32[]{:S(2)}) async-start(bf16[128,16,768]{2,1,0:T(8,128)(2,1)} %select_convert_fusion), calls=%async_computation.2 | async-start | bytes 6291456 | tf_op jit(solution)/shard_map/all_to_all | solution.py:77
  76.4 2.4 reduce.2
  79.7 5.8 %gather_fusion.2 = bf16[1024,256]{1,0:T(8,128)(2,1)} fusion(f32[1024,256]{1,0:T(8,128)} %param.15, s32[1024]{0:T(1024)S(1)} %broadcast_clamp_fusion.1), kind=kCustom, calls=%fused_computation.2 | custom fusion | bytes 1052672 | tf_op jit(solution)/shard_map/gather | solution.py:72
  85.6 2.0 fusion.9
  87.6 30.1 %all-to-all-done.2 = bf16[128,16,768]{2,1,0:T(8,128)(2,1)} async-done(((bf16[128,16,768]{2,1,0:T(8,128)(2,1)}), bf16[128,16,768]{2,1,0:T(8,128)(2,1)}, u32[]{:S(2)}, u32[]{:S(2)}) %all-to-all-start.2) | async-done | bytes 3145760 | tf_op jit(solution)/shard_map/all_to_all | solution.py:77
  117.7 5.6 %all-to-all-start.5 = ((bf16[128,8,256]{2,1,0:T(8,128)(2,1)}), bf16[128,8,256]{2,1,0:T(8,128)(2,1)}, u32[]{:S(2)}, u32[]{:S(2)}) async-start(bf16[128,8,256]{2,1,0:T(8,128)(2,1)} %fusion.9), calls=%async_computation.5 | async-start | bytes 1048576 | tf_op jit(solution)/shard_map/all_to_all | solution.py:74
  123.4 4.0 fusion.6
  127.3 1.6 copy.26
  128.9 8.0 %all-to-all-done.5 = bf16[128,8,256]{2,1,0:T(8,128)(2,1)} async-done(((bf16[128,8,256]{2,1,0:T(8,128)(2,1)}), bf16[128,8,256]{2,1,0:T(8,128)(2,1)}, u32[]{:S(2)}, u32[]{:S(2)}) %all-to-all-start.5) | async-done | bytes 524320 | tf_op jit(solution)/shard_map/all_to_all | solution.py:74
  136.9 2.7 pad_maximum_fusion
  139.5 1.6 broadcast_in_dim.38
  141.1 264.6 %while.10 = (s32[]{:T(128)}, f32[16,128,256]{2,1,0:T(8,128)}, s32[8]{0:T(128)S(1)}, s32[512]{0:T(512)}, bf16[512,128,128]{2,1,0:T(8,128)(2,1)}, /*index=5*/s32[5...) while((s32[]{:T(128)}, f32[16,128,256]{2,1,0:T(8,128)}, ...), condition=%wide.region_2.3_spmd, body=%wide.region_0.2_spmd.sunk | while | flops 541066816 | bytes 48241096 | solution.py:31
  143.8 4.2 %gather_fusion = bf16[64,128,256]{2,1,0:T(8,128)(2,1)} fusion(bf16[24,128,256]{2,1,0:T(8,128)(2,1)} %get-tuple-element.149, s32[1024]{0:T(1024)S(1)} %pad_clamp_fusion.2), kind=kCustom, calls=%fused_computation.clone.1 | custom fusion | bytes 8388864 | tf_op jit(solution)/shard_map/while/body/eval_jaxpr/gather | solution.py:21
  148.0 7.3 %broadcast_multiply_fusion.2 = f32[64,128,256]{2,1,0:T(8,128)} fusion(f32[64]{0:T(128)S(1)} %compare_convert_fusion.2, bf16[64,128,256]{2,1,0:T(8,128)(2,1)} %gather_fusion, bf16[512,128,128]{2,1,0:T(8,128)(2,1)} %get-tuple-element.147, s32[]{:T(128)S(6)} %select_n.56), kind=kOutput, calls=%fused_computation.4.clone.1 | convolution fusion | flops 538968064 | bytes 14680324 | tf_op jit(solution)/shard_map/while/body/eval_jaxpr/gij,gjk->gik/dot_general | solution.py:22
  155.3 18.8 %scatter_fusion = f32[16,128,256]{2,1,0:T(8,128)} fusion(f32[16,128,256]{2,1,0:T(8,128)} %get-tuple-element.132, s32[64]{0:T(128)S(1)} %get-tuple-element.117, f32[64,128,256]{2,1,0:T(8,128)} %broadcast_multiply_fusion.2), kind=kCustom, calls=%fused_computation.3.clone.1 | custom fusion | flops 2097152 | bytes 25166080 | tf_op jit(solution)/shard_map/while/body/eval_jaxpr/scatter-add | solution.py:27
  176.8 4.2 %gather_fusion = bf16[64,128,256]{2,1,0:T(8,128)(2,1)} fusion(bf16[24,128,256]{2,1,0:T(8,128)(2,1)} %get-tuple-element.149, s32[1024]{0:T(1024)S(1)} %pad_clamp_fusion.2), kind=kCustom, calls=%fused_computation.clone.1 | custom fusion | bytes 8388864 | tf_op jit(solution)/shard_map/while/body/eval_jaxpr/gather | solution.py:21
  181.0 7.3 %broadcast_multiply_fusion.2 = f32[64,128,256]{2,1,0:T(8,128)} fusion(f32[64]{0:T(128)S(1)} %compare_convert_fusion.2, bf16[64,128,256]{2,1,0:T(8,128)(2,1)} %gather_fusion, bf16[512,128,128]{2,1,0:T(8,128)(2,1)} %get-tuple-element.147, s32[]{:T(128)S(6)} %select_n.56), kind=kOutput, calls=%fused_computation.4.clone.1 | convolution fusion | flops 538968064 | bytes 14680324 | tf_op jit(solution)/shard_map/while/body/eval_jaxpr/gij,gjk->gik/dot_general | solution.py:22
  188.3 18.9 %scatter_fusion = f32[16,128,256]{2,1,0:T(8,128)} fusion(f32[16,128,256]{2,1,0:T(8,128)} %get-tuple-element.132, s32[64]{0:T(128)S(1)} %get-tuple-element.117, f32[64,128,256]{2,1,0:T(8,128)} %broadcast_multiply_fusion.2), kind=kCustom, calls=%fused_computation.3.clone.1 | custom fusion | flops 2097152 | bytes 25166080 | tf_op jit(solution)/shard_map/while/body/eval_jaxpr/scatter-add | solution.py:27
  209.9 4.2 %gather_fusion = bf16[64,128,256]{2,1,0:T(8,128)(2,1)} fusion(bf16[24,128,256]{2,1,0:T(8,128)(2,1)} %get-tuple-element.149, s32[1024]{0:T(1024)S(1)} %pad_clamp_fusion.2), kind=kCustom, calls=%fused_computation.clone.1 | custom fusion | bytes 8388864 | tf_op jit(solution)/shard_map/while/body/eval_jaxpr/gather | solution.py:21
  214.1 7.3 %broadcast_multiply_fusion.2 = f32[64,128,256]{2,1,0:T(8,128)} fusion(f32[64]{0:T(128)S(1)} %compare_convert_fusion.2, bf16[64,128,256]{2,1,0:T(8,128)(2,1)} %gather_fusion, bf16[512,128,128]{2,1,0:T(8,128)(2,1)} %get-tuple-element.147, s32[]{:T(128)S(6)} %select_n.56), kind=kOutput, calls=%fused_computation.4.clone.1 | convolution fusion | flops 538968064 | bytes 14680324 | tf_op jit(solution)/shard_map/while/body/eval_jaxpr/gij,gjk->gik/dot_general | solution.py:22
  221.4 18.9 %scatter_fusion = f32[16,128,256]{2,1,0:T(8,128)} fusion(f32[16,128,256]{2,1,0:T(8,128)} %get-tuple-element.132, s32[64]{0:T(128)S(1)} %get-tuple-element.117, f32[64,128,256]{2,1,0:T(8,128)} %broadcast_multiply_fusion.2), kind=kCustom, calls=%fused_computation.3.clone.1 | custom fusion | flops 2097152 | bytes 25166080 | tf_op jit(solution)/shard_map/while/body/eval_jaxpr/scatter-add | solution.py:27
  243.1 4.2 %gather_fusion = bf16[64,128,256]{2,1,0:T(8,128)(2,1)} fusion(bf16[24,128,256]{2,1,0:T(8,128)(2,1)} %get-tuple-element.149, s32[1024]{0:T(1024)S(1)} %pad_clamp_fusion.2), kind=kCustom, calls=%fused_computation.clone.1 | custom fusion | bytes 8388864 | tf_op jit(solution)/shard_map/while/body/eval_jaxpr/gather | solution.py:21
  247.2 7.3 %broadcast_multiply_fusion.2 = f32[64,128,256]{2,1,0:T(8,128)} fusion(f32[64]{0:T(128)S(1)} %compare_convert_fusion.2, bf16[64,128,256]{2,1,0:T(8,128)(2,1)} %gather_fusion, bf16[512,128,128]{2,1,0:T(8,128)(2,1)} %get-tuple-element.147, s32[]{:T(128)S(6)} %select_n.56), kind=kOutput, calls=%fused_computation.4.clone.1 | convolution fusion | flops 538968064 | bytes 14680324 | tf_op jit(solution)/shard_map/while/body/eval_jaxpr/gij,gjk->gik/dot_general | solution.py:22
  254.5 18.9 %scatter_fusion = f32[16,128,256]{2,1,0:T(8,128)} fusion(f32[16,128,256]{2,1,0:T(8,128)} %get-tuple-element.132, s32[64]{0:T(128)S(1)} %get-tuple-element.117, f32[64,128,256]{2,1,0:T(8,128)} %broadcast_multiply_fusion.2), kind=kCustom, calls=%fused_computation.3.clone.1 | custom fusion | flops 2097152 | bytes 25166080 | tf_op jit(solution)/shard_map/while/body/eval_jaxpr/scatter-add | solution.py:27
  276.2 4.2 %gather_fusion = bf16[64,128,256]{2,1,0:T(8,128)(2,1)} fusion(bf16[24,128,256]{2,1,0:T(8,128)(2,1)} %get-tuple-element.149, s32[1024]{0:T(1024)S(1)} %pad_clamp_fusion.2), kind=kCustom, calls=%fused_computation.clone.1 | custom fusion | bytes 8388864 | tf_op jit(solution)/shard_map/while/body/eval_jaxpr/gather | solution.py:21
  280.4 7.3 %broadcast_multiply_fusion.2 = f32[64,128,256]{2,1,0:T(8,128)} fusion(f32[64]{0:T(128)S(1)} %compare_convert_fusion.2, bf16[64,128,256]{2,1,0:T(8,128)(2,1)} %gather_fusion, bf16[512,128,128]{2,1,0:T(8,128)(2,1)} %get-tuple-element.147, s32[]{:T(128)S(6)} %select_n.56), kind=kOutput, calls=%fused_computation.4.clone.1 | convolution fusion | flops 538968064 | bytes 14680324 | tf_op jit(solution)/shard_map/while/body/eval_jaxpr/gij,gjk->gik/dot_general | solution.py:22
  287.7 18.8 %scatter_fusion = f32[16,128,256]{2,1,0:T(8,128)} fusion(f32[16,128,256]{2,1,0:T(8,128)} %get-tuple-element.132, s32[64]{0:T(128)S(1)} %get-tuple-element.117, f32[64,128,256]{2,1,0:T(8,128)} %broadcast_multiply_fusion.2), kind=kCustom, calls=%fused_computation.3.clone.1 | custom fusion | flops 2097152 | bytes 25166080 | tf_op jit(solution)/shard_map/while/body/eval_jaxpr/scatter-add | solution.py:27
  309.2 4.2 %gather_fusion = bf16[64,128,256]{2,1,0:T(8,128)(2,1)} fusion(bf16[24,128,256]{2,1,0:T(8,128)(2,1)} %get-tuple-element.149, s32[1024]{0:T(1024)S(1)} %pad_clamp_fusion.2), kind=kCustom, calls=%fused_computation.clone.1 | custom fusion | bytes 8388864 | tf_op jit(solution)/shard_map/while/body/eval_jaxpr/gather | solution.py:21
  313.4 7.3 %broadcast_multiply_fusion.2 = f32[64,128,256]{2,1,0:T(8,128)} fusion(f32[64]{0:T(128)S(1)} %compare_convert_fusion.2, bf16[64,128,256]{2,1,0:T(8,128)(2,1)} %gather_fusion, bf16[512,128,128]{2,1,0:T(8,128)(2,1)} %get-tuple-element.147, s32[]{:T(128)S(6)} %select_n.56), kind=kOutput, calls=%fused_computation.4.clone.1 | convolution fusion | flops 538968064 | bytes 14680324 | tf_op jit(solution)/shard_map/while/body/eval_jaxpr/gij,gjk->gik/dot_general | solution.py:22
  320.7 18.9 %scatter_fusion = f32[16,128,256]{2,1,0:T(8,128)} fusion(f32[16,128,256]{2,1,0:T(8,128)} %get-tuple-element.132, s32[64]{0:T(128)S(1)} %get-tuple-element.117, f32[64,128,256]{2,1,0:T(8,128)} %broadcast_multiply_fusion.2), kind=kCustom, calls=%fused_computation.3.clone.1 | custom fusion | flops 2097152 | bytes 25166080 | tf_op jit(solution)/shard_map/while/body/eval_jaxpr/scatter-add | solution.py:27
  342.3 4.2 %gather_fusion = bf16[64,128,256]{2,1,0:T(8,128)(2,1)} fusion(bf16[24,128,256]{2,1,0:T(8,128)(2,1)} %get-tuple-element.149, s32[1024]{0:T(1024)S(1)} %pad_clamp_fusion.2), kind=kCustom, calls=%fused_computation.clone.1 | custom fusion | bytes 8388864 | tf_op jit(solution)/shard_map/while/body/eval_jaxpr/gather | solution.py:21
  346.5 7.3 %broadcast_multiply_fusion.2 = f32[64,128,256]{2,1,0:T(8,128)} fusion(f32[64]{0:T(128)S(1)} %compare_convert_fusion.2, bf16[64,128,256]{2,1,0:T(8,128)(2,1)} %gather_fusion, bf16[512,128,128]{2,1,0:T(8,128)(2,1)} %get-tuple-element.147, s32[]{:T(128)S(6)} %select_n.56), kind=kOutput, calls=%fused_computation.4.clone.1 | convolution fusion | flops 538968064 | bytes 14680324 | tf_op jit(solution)/shard_map/while/body/eval_jaxpr/gij,gjk->gik/dot_general | solution.py:22
  353.8 18.8 %scatter_fusion = f32[16,128,256]{2,1,0:T(8,128)} fusion(f32[16,128,256]{2,1,0:T(8,128)} %get-tuple-element.132, s32[64]{0:T(128)S(1)} %get-tuple-element.117, f32[64,128,256]{2,1,0:T(8,128)} %broadcast_multiply_fusion.2), kind=kCustom, calls=%fused_computation.3.clone.1 | custom fusion | flops 2097152 | bytes 25166080 | tf_op jit(solution)/shard_map/while/body/eval_jaxpr/scatter-add | solution.py:27
  375.3 4.2 %gather_fusion = bf16[64,128,256]{2,1,0:T(8,128)(2,1)} fusion(bf16[24,128,256]{2,1,0:T(8,128)(2,1)} %get-tuple-element.149, s32[1024]{0:T(1024)S(1)} %pad_clamp_fusion.2), kind=kCustom, calls=%fused_computation.clone.1 | custom fusion | bytes 8388864 | tf_op jit(solution)/shard_map/while/body/eval_jaxpr/gather | solution.py:21
  379.5 7.3 %broadcast_multiply_fusion.2 = f32[64,128,256]{2,1,0:T(8,128)} fusion(f32[64]{0:T(128)S(1)} %compare_convert_fusion.2, bf16[64,128,256]{2,1,0:T(8,128)(2,1)} %gather_fusion, bf16[512,128,128]{2,1,0:T(8,128)(2,1)} %get-tuple-element.147, s32[]{:T(128)S(6)} %select_n.56), kind=kOutput, calls=%fused_computation.4.clone.1 | convolution fusion | flops 538968064 | bytes 14680324 | tf_op jit(solution)/shard_map/while/body/eval_jaxpr/gij,gjk->gik/dot_general | solution.py:22
  386.8 18.9 %scatter_fusion = f32[16,128,256]{2,1,0:T(8,128)} fusion(f32[16,128,256]{2,1,0:T(8,128)} %get-tuple-element.132, s32[64]{0:T(128)S(1)} %get-tuple-element.117, f32[64,128,256]{2,1,0:T(8,128)} %broadcast_multiply_fusion.2), kind=kCustom, calls=%fused_computation.3.clone.1 | custom fusion | flops 2097152 | bytes 25166080 | tf_op jit(solution)/shard_map/while/body/eval_jaxpr/scatter-add | solution.py:27
  405.7 1.8 convert_element_type.33
  (55 shorter events, 24.9 us)
Async XLA Ops:
  0.0 42.7 %copy-start = (f32[1024,768]{1,0:T(8,128)S(1)}, f32[1024,768]{1,0:T(8,128)}, u32[]{:S(2)}) copy-start(f32[1024,768]{1,0:T(8,128)} %param.14) | copy-start | bytes 9437188
  1.5 21.1 %all-to-all-start = ((s32[128,1,1]{2,1,0:T(1,128)}), s32[128,1,1]{2,1,0:T(1,128)S(1)}, u32[]{:S(2)}, u32[]{:S(2)}) async-start(s32[128,1,1]{2,1,0:T(1,128)} %copy.23), calls=%async_computation | async-start | bytes 131072 | tf_op jit(solution)/shard_map/all_to_all | solution.py:58
  22.7 14.1 %all-to-all-start.1 = ((s32[128,1,16]{2,1,0:T(1,128)}), s32[128,1,16]{2,1,0:T(1,128)S(1)}, u32[]{:S(2)}, u32[]{:S(2)}) async-start(s32[128,1,16]{2,1,0:T(1,128)} %bitcast.2), calls=%async_computation.1 | async-start | bytes 131072 | tf_op jit(solution)/shard_map/all_to_all | solution.py:57
  36.8 15.0 %all-to-all-start.3 = ((s32[128,1,1]{2,1,0:T(1,128)}), s32[128,1,1]{2,1,0:T(1,128)S(1)}, u32[]{:S(2)}, u32[]{:S(2)}) async-start(s32[128,1,1]{2,1,0:T(1,128)} %copy.27), calls=%async_computation.3 | async-start | bytes 131072 | tf_op jit(solution)/shard_map/all_to_all | solution.py:62
  51.8 19.3 %all-to-all-start.4 = ((s32[128,1,8]{2,1,0:T(1,128)}), s32[128,1,8]{2,1,0:T(1,128)S(1)}, u32[]{:S(2)}, u32[]{:S(2)}) async-start(s32[128,1,8]{2,1,0:T(1,128)} %bitcast.8), calls=%async_computation.4 | async-start | bytes 131072 | tf_op jit(solution)/shard_map/all_to_all | solution.py:61
  71.1 46.6 %all-to-all-start.2 = ((bf16[128,16,768]{2,1,0:T(8,128)(2,1)}), bf16[128,16,768]{2,1,0:T(8,128)(2,1)}, u32[]{:S(2)}, u32[]{:S(2)}) async-start(bf16[128,16,768]{2,1,0:T(8,128)(2,1)} %select_convert_fusion), calls=%async_computation.2 | async-start | bytes 6291456 | tf_op jit(solution)/shard_map/all_to_all | solution.py:77
  117.7 19.1 %all-to-all-start.5 = ((bf16[128,8,256]{2,1,0:T(8,128)(2,1)}), bf16[128,8,256]{2,1,0:T(8,128)(2,1)}, u32[]{:S(2)}, u32[]{:S(2)}) async-start(bf16[128,8,256]{2,1,0:T(8,128)(2,1)} %fusion.9), calls=%async_computation.5 | async-start | bytes 1048576 | tf_op jit(solution)/shard_map/all_to_all | solution.py:74
  405.7 1.9 copy-start.1
  405.7 1.9 copy-start.2
where the time goes:
time: 411 us; the launch traced here: 409 us
  other arithmetic  179 us (44%)
  matrix products  63.7 us (15%)
  local copies, waits for them, and re-layouts  63.1 us (15%)
  waiting for transfers between devices  56.7 us (14%)
  starting transfers between devices  41.1 us (10%)
  loops' own time  5.25 us (1%)
    scatter-add x8, other arithmetic, add_group(): running = running.at[rows_group].add(products * live_tiles[:, None, None])  151 us
    dot_general x8, matrix products, add_group(): jnp.einsum('gij,gjk->gik', vals_group, picked, preferred_element_type=jnp...  58.3 us
    gather x8, local copies, waits for them, and re-layouts, add_group(): picked = blocks[cols_group]  33.4 us
    all_to_all x1, waiting for transfers between devices, on_device(): lax.all_to_all(picked_rows, 'nodes', split_axis=0, concat_axis=0, tiled=T...  30.1 us
    all_to_all x1, starting transfers between devices, on_device(): lax.all_to_all(wanted_count, 'nodes', split_axis=0, concat_axis=0, tiled=...  11.5 us
    all_to_all x1, starting transfers between devices, on_device(): lax.all_to_all(halo_wanted, 'nodes', split_axis=0, concat_axis=0, tiled=T...  9.76 us
    gather x1, local copies, waits for them, and re-layouts, on_device(): features[asked.reshape(-1)]  9.08 us
  transfers between devices with their start and end apart: 6, of which 5 were waited for; matrix products, arithmetic and copies ran while one was open for 9% of the time, Pallas kernels for 0%

commit v1 on v0

v1 whole, which is shorter than its diff:
```python
import functools

import jax
import jax.numpy as jnp
from jax import lax
from jax.experimental import pallas as pl
from jax.experimental.pallas import tpu as pltpu
from jax.sharding import PartitionSpec as P

LANES = 128
TILE_STEP = 32
OWNERS_STEP = 16
ROWS_STEP = 512


def pack_kernel(req_ref, halo_ref, req_count_ref, halo_count_ref, out_ref):
    req = req_ref[...]
    halo = halo_ref[...]
    req_slot = lax.broadcasted_iota(jnp.int32, req.shape, 0)
    halo_slot = lax.broadcasted_iota(jnp.int32, halo.shape, 0)
    req = jnp.where(req_slot < req_count_ref[...], req, -1)
    halo = jnp.where(halo_slot < halo_count_ref[...], halo, -1)
    rest = jnp.full((LANES - req.shape[0] - halo.shape[0], req.shape[1]), -1, jnp.int32)
    out_ref[...] = jnp.concatenate([req, halo, rest], axis=0).T


def pack_ids(req_t, halo_t, req_count, halo_count):
    owners = req_t.shape[1]
    return pl.pallas_call(
        pack_kernel,
        out_shape=jax.ShapeDtypeStruct((owners, LANES), jnp.int32),
        name="pack_ids",
    )(req_t, halo_t, req_count, halo_count)


def pick_kernel(req, halo, ids_ref, proj_ref, hist_ref, out_ref, turned_ref):
    count = ids_ref.shape[0]
    rows = proj_ref.shape[0]
    turned_ref[...] = ids_ref[...].T[: req + halo]
    group = OWNERS_STEP

    def one_hot(columns, start, size):
        wanted = jnp.concatenate(
            [columns[start : start + size, j : j + 1] for j in range(group)], axis=0
        )
        wide = jnp.broadcast_to(wanted, (size * group, LANES))
        lane = lax.broadcasted_iota(jnp.int32, wide.shape, 1)
        parts = [
            jnp.where(wide == lane + k * LANES, 1.0, 0.0).astype(jnp.bfloat16)
            for k in range(rows // LANES)
        ]
        return jnp.concatenate(parts, axis=1)

    @pl.loop(0, count // group)
    def _(g):
        columns = pltpu.roll(turned_ref[...], lax.rem(count - g * group, count), 1)
        at = pl.ds(g * group, group)
        picked = jnp.dot(
            one_hot(columns, 0, req), proj_ref[...], preferred_element_type=jnp.float32
        ).astype(jnp.bfloat16)
        out_ref[at, :req, :] = picked.reshape(group, req, -1)
        picked = jnp.dot(
            one_hot(columns, req, halo), hist_ref[...], preferred_element_type=jnp.float32
        ).astype(jnp.bfloat16)
        out_ref[at, req:, :] = picked.reshape(group, halo, -1)


def pick_rows(ids, proj, hist, req, halo):
    count = ids.shape[0]
    hidden = proj.shape[1]
    flops = 2 * count * (req + halo) * proj.shape[0] * hidden
    return pl.pallas_call(
        functools.partial(pick_kernel, req, halo),
        out_shape=jax.ShapeDtypeStruct((count, req + halo, hidden), jnp.bfloat16),
        scratch_shapes=[pltpu.VMEM((req + halo, count), jnp.int32)],
        cost_estimate=pl.CostEstimate(flops=flops, bytes_accessed=3 << 20, transcendentals=0),
        name="pick_rows",
    )(ids, proj, hist)


def dense_kernel(col_blocks, fill_steps, rows_ref, cols_ref, used_ref, tiles_ref, out_ref, acc_ref):
    i = pl.program_id(0)
    side = tiles_ref.shape[1]

    @pl.when(i == 0)
    def _():
        @pl.loop(0, acc_ref.shape[0])
        def _(b):
            acc_ref[b] = jnp.zeros(acc_ref.shape[1:], jnp.float32)

    @pl.when(i < fill_steps)
    def _():
        first = i * TILE_STEP
        live = jnp.clip(used_ref[0] - first, 0, TILE_STEP)

        @pl.loop(0, live)
        def _(t):
            block = rows_ref[first + t] * col_blocks + cols_ref[first + t]
            acc_ref[block] = acc_ref[block] + tiles_ref[t].astype(jnp.float32)

    @pl.when(i >= fill_steps)
    def _():
        base = (i - fill_steps) * col_blocks
        for c in range(col_blocks):
            out_ref[:, c * side : (c + 1) * side] = acc_ref[base + c].astype(jnp.bfloat16)


def build_dense(tile_rows, tile_cols, tile_count, tile_values, row_blocks, col_blocks):
    slots, side, _ = tile_values.shape
    fill_steps = slots // TILE_STEP
    last = fill_steps - 1
    return pl.pallas_call(
        functools.partial(dense_kernel, col_blocks, fill_steps),
        grid_spec=pltpu.PrefetchScalarGridSpec(
            num_scalar_prefetch=3,
            grid=(fill_steps + row_blocks,),
            in_specs=[
                pl.BlockSpec(
                    (TILE_STEP, side, side), lambda i, *_: (jnp.minimum(i, last), 0, 0)
                )
            ],
            out_specs=pl.BlockSpec(
                (side, col_blocks * side), lambda i, *_: (jnp.maximum(i - fill_steps, 0), 0)
            ),
            scratch_shapes=[pltpu.VMEM((row_blocks * col_blocks, side, side), jnp.float32)],
        ),
        out_shape=jax.ShapeDtypeStruct((row_blocks * side, col_blocks * side), jnp.bfloat16),
        compiler_params=pltpu.CompilerParams(vmem_limit_bytes=36 << 20),
        cost_estimate=pl.CostEstimate(flops=1 << 20, bytes_accessed=30 << 20, transcendentals=0),
        name="build_dense",
    )(tile_rows, tile_cols, tile_count, tile_values)


def combine_kernel(req, dense_ref, came_ref, w_ref, out_ref, source_ref):
    i = pl.program_id(0)
    owners, slots, hidden = came_ref.shape
    nodes = owners * req

    @pl.when(i == 0)
    def _():
        source_ref[:nodes] = came_ref[:, :req, :].reshape(nodes, hidden)
        source_ref[nodes:] = came_ref[:, req:, :].reshape(owners * (slots - req), hidden)

    total = jnp.dot(dense_ref[...], source_ref[...], preferred_element_type=jnp.float32)
    mixed = jnp.dot(total.astype(jnp.bfloat16), w_ref[...], preferred_element_type=jnp.float32)
    own = source_ref[pl.ds(i * out_ref.shape[0], out_ref.shape[0]), :].astype(jnp.float32)
    out_ref[...] = jnp.maximum(mixed + own, 0.0).astype(jnp.bfloat16)


def combine(dense, came, w_out, req):
    owners, slots, hidden = came.shape
    nodes, width = dense.shape
    step = ROWS_STEP
    return pl.pallas_call(
        functools.partial(combine_kernel, req),
        grid=(nodes // step,),
        in_specs=[
            pl.BlockSpec((step, width), lambda i: (i, 0)),
            pl.BlockSpec((owners, slots, hidden), lambda i: (0, 0, 0)),
            pl.BlockSpec((hidden, hidden), lambda i: (0, 0)),
        ],
        out_specs=pl.BlockSpec((step, hidden), lambda i: (i, 0)),
        out_shape=jax.ShapeDtypeStruct((nodes, hidden), jnp.bfloat16),
        scratch_shapes=[pltpu.VMEM((width, hidden), jnp.bfloat16)],
        cost_estimate=pl.CostEstimate(
            flops=2 * nodes * width * hidden, bytes_accessed=16 << 20, transcendentals=0
        ),
        compiler_params=pltpu.CompilerParams(vmem_limit_bytes=24 << 20),
        name="combine",
    )(dense, came, w_out)


def on_device(
    features,
    history,
    request_ids,
    request_count,
    halo_ids,
    halo_count,
    tile_values,
    tile_rows,
    tile_cols,
    tile_count,
    w_in,
    w_out,
):
    owners, req = request_ids.shape[1:]
    halo = halo_ids.shape[2]
    side = tile_values.shape[1]
    wanted = pack_ids(request_ids[0].T, halo_ids[0].T, request_count, halo_count)
    asked = lax.all_to_all(wanted, "nodes", split_axis=0, concat_axis=0, tiled=True)
    proj = jnp.dot(
        features.astype(jnp.bfloat16), w_in, preferred_element_type=jnp.float32
    ).astype(jnp.bfloat16)
    picked = pick_rows(asked, proj, history.astype(jnp.bfloat16), req, halo)
    picked, tile_count = lax.optimization_barrier((picked, tile_count))
    came = lax.all_to_all(picked, "nodes", split_axis=0, concat_axis=0, tiled=True)
    dense = build_dense(
        tile_rows, tile_cols, tile_count, tile_values,
        owners * req // side, owners * (req + halo) // side,
    )
    return combine(dense, came, w_out, req)


def solution(mesh):
    in_specs = (
        P("nodes", None),
        P("nodes", None),
        P("nodes", None, None),
        P("nodes", None),
        P("nodes", None, None),
        P("nodes", None),
        P("nodes", None, None),
        P("nodes"),
        P("nodes"),
        P("nodes"),
        P(),
        P(),
    )
    out_specs = P("nodes", None)
    return jax.shard_map(
        on_device, mesh=mesh, in_specs=in_specs, out_specs=out_specs, check_vma=False
    )
```

time: 411 us -> 70.8 us (0.17)
  other arithmetic: 179 us -> 0.84 us
  matrix products: 63.7 us -> 3.26 us
  local copies, waits for them, and re-layouts: 63.1 us -> 9.73 us
  waiting for transfers between devices: 56.7 us -> 7.33 us
  Pallas kernels: 0 us -> 32.4 us
  starting transfers between devices: 41.1 us -> 16 us
  loops' own time: 5.25 us -> 0 us
    scatter-add x8 -> x0, other arithmetic: 151 us -> none  [add_group(): running = running.at[rows_group].add(products * live_tiles[:, None, None])]
    dot_general x10 -> x1, matrix products: 63.7 us -> 3.26 us  [on_device(): jnp.dot(features.astype(jnp.bfloat16), w_in, preferred_element_type=jnp.f...]
    gather x10 -> x0, local copies, waits for them, and re-layouts: 48.3 us -> none  [the longest x8 33.4 us: add_group(): picked = blocks[cols_group]]
    all_to_all x5 -> x1, waiting for transfers between devices: 49.6 us -> 1.84 us  [on_device(): lax.all_to_all(picked, 'nodes', split_axis=0, concat_axis=0, tiled=True)]
    pallas_call x0 -> x4, Pallas kernels: none -> 32.4 us  [the longest x1 17.9 us: build_dense(): pl.pallas_call(functools.partial(dense_kernel, col_blocks, fill_steps), g...]
    all_to_all x5 -> x1, starting transfers between devices: 36.6 us -> 4.5 us  [on_device(): lax.all_to_all(picked, 'nodes', split_axis=0, concat_axis=0, tiled=True)]
    convert_element_type x11 -> x1, other arithmetic: 12.5 us -> 0.84 us  [on_device(): picked = pick_rows(asked, proj, history.astype(jnp.bfloat16), req, halo)]
    all_to_all x1, starting transfers between devices: 4.5 us -> 11.5 us  [on_device(): lax.all_to_all(wanted, 'nodes', split_axis=0, concat_axis=0, tiled=True)]
  transfers between devices with their start and end apart: 6 -> 2, of which waited for: 5 -> 2; matrix products, arithmetic and copies ran while one was open for 9% -> 6% of each run, Pallas kernels for 0% -> 25%
where the time goes in v1:
time: 70.8 us; the launch traced here: 70.3 us
  Pallas kernels  32.4 us (46%)
  starting transfers between devices  16 us (23%)
  local copies, waits for them, and re-layouts  9.73 us (14%)
  waiting for transfers between devices  7.33 us (10%)
  matrix products  3.26 us (5%)
  other arithmetic  0.84 us (1%)
  between operations  0.72 us (1%)
    pallas_call x1, Pallas kernels, build_dense(): pl.pallas_call(functools.partial(dense_kernel, col_blocks, fill_steps), g...  17.9 us
    all_to_all x1, starting transfers between devices, on_device(): lax.all_to_all(wanted, 'nodes', split_axis=0, concat_axis=0, tiled=True)  11.5 us
    unnamed x16, local copies, waits for them, and re-layouts  9.73 us
    pallas_call x1, Pallas kernels, pick_rows(): pl.pallas_call(functools.partial(pick_kernel, req, halo), out_shape=jax.S...  7.43 us
    pallas_call x1, Pallas kernels, combine(): pl.pallas_call(functools.partial(combine_kernel, req), grid=(nodes // ste...  5.54 us
    all_to_all x1, waiting for transfers between devices, on_device(): lax.all_to_all(wanted, 'nodes', split_axis=0, concat_axis=0, tiled=True)  5.49 us
    all_to_all x1, starting transfers between devices, on_device(): lax.all_to_all(picked, 'nodes', split_axis=0, concat_axis=0, tiled=True)  4.5 us
    dot_general x1, matrix products, on_device(): jnp.dot(features.astype(jnp.bfloat16), w_in, preferred_element_type=jnp.f...  3.26 us
  transfers between devices with their start and end apart: 2, of which 2 were waited for; matrix products, arithmetic and copies ran while one was open for 6% of the time, Pallas kernels for 25%

profile of v1, /device:TPU:1, one launch (start us, length us, event | category | flops | bytes accessed | tf_op | source)
XLA Modules:
  0.0 70.3 jit_solution(7365139258393423735)
XLA Ops:
  0.0 0.0 copy-start
  0.0 0.0 copy-start.6
  0.0 1.5 %pack_ids.1 = s32[128,128]{1,0:T(8,128)} custom-call(s32[16,128]{1,0:T(8,128)} %bitcast.13, s32[8,128]{1,0:T(8,128)} %bitcast.14, s32[1,128]{1,0:T(1,128)} %req_count_ref.1, s32[1,128]{1,0:T(1,128)} %halo_count_ref.1), custom_call_target="tpu_custom_call" | custom-call | tf_op jit(solution)/shard_map/pack_ids/pallas_call | solution.py:29
  1.6 11.5 %all-to-all-start = ((s32[128,1,128]{2,1,0:T(1,128)}), s32[128,1,128]{2,1,0:T(1,128)S(1)}, u32[]{:S(2)}, u32[]{:S(2)}) async-start(s32[128,1,128]{2,1,0:T(1,128)} %bitcast.11), calls=%async_computation | async-start | bytes 131072 | tf_op jit(solution)/shard_map/all_to_all | solution.py:191
  13.1 0.0 copy-done
  13.1 3.3 %fusion.2.proj_ref = bf16[1024,256]{1,0:T(8,128)(2,1)} fusion(bf16[768,256]{1,0:T(8,128)(2,1)S(1)} %copy-done, f32[1024,768]{1,0:T(8,128)} %param.12), kind=kOutput, calls=%fused_computation.2 | convolution fusion | flops 403701760 | bytes 4063232 | tf_op jit(solution)/shard_map/dot_general | solution.py:192
  16.3 0.0 copy-done.6
  16.3 0.8 %convert_element_type.11.hist_ref = bf16[1024,256]{1,0:T(8,128)(2,1)} convert(f32[1024,256]{1,0:T(8,128)S(1)} %copy-done.6) | non-fusion elementwise | flops 262144 | bytes 1572864 | tf_op jit(solution)/shard_map/convert_element_type | solution.py:195
  17.2 5.5 %all-to-all-done = s32[128,1,128]{2,1,0:T(1,128)S(1)} async-done(((s32[128,1,128]{2,1,0:T(1,128)}), s32[128,1,128]{2,1,0:T(1,128)S(1)}, u32[]{:S(2)}, u32[]{:S(2)}) %all-to-all-start) | async-done | bytes 65568 | tf_op jit(solution)/shard_map/all_to_all | solution.py:191
  22.7 0.0 copy-start.7
  22.7 0.6 copy-done.7
  23.3 0.0 copy-start.4
  23.3 0.0 copy-start.5
  23.3 7.4 %pick_rows.1 = bf16[128,24,256]{2,1,0:T(8,128)(2,1)} custom-call(s32[128,128]{1,0:T(8,128)} %bitcast.12, bf16[1024,256]{1,0:T(8,128)(2,1)} %fusion.2.proj_ref, bf16[1024,256]{1,0:T(8,128)(2,1)} %convert_element_type.11.hist_ref), custom_call_target="tpu_custom_call" | custom-call | flops 1610612736 | bytes 3145728 | tf_op jit(solution)/shard_map/pick_rows/pallas_call | solution.py:72
  30.7 4.5 %all-to-all-start.1 = ((bf16[128,24,256]{2,1,0:T(8,128)(2,1)}), bf16[128,24,256]{2,1,0:T(8,128)(2,1)S(1)}, u32[]{:S(2)}, u32[]{:S(2)}) async-start(bf16[128,24,256]{2,1,0:T(8,128)(2,1)} %pick_rows.1), calls=%async_computation.1 | async-start | bytes 3145728 | tf_op jit(solution)/shard_map/all_to_all | solution.py:197
  35.9 0.0 copy-done.4
  35.9 0.0 copy-done.5
  35.9 0.0 copy-start.3
  35.9 17.9 %build_dense.1.dense_ref = bf16[2048,3072]{1,0:T(8,128)(2,1)S(1)} custom-call(s32[512]{0:T(512)S(1)} %copy-done.4, s32[512]{0:T(512)S(1)} %copy-done.5, s32[1]{0:T(128)S(6)} %copy.14.used_ref, bf16[512,128,128]{2,1,0:T(8,128)(2,1)} %tiles_ref.1), custom_call_target="tpu_custom_call" | custom-call | flops 1048576 | bytes 31457280 | tf_op jit(solution)/shard_map/build_dense/pallas_call | solution.py:112
  53.8 0.0 copy-start.1
  53.8 4.5 %copy-done.1 = bf16[2048,3072]{1,0:T(8,128)(2,1)} copy-done((bf16[2048,3072]{1,0:T(8,128)(2,1)}, bf16[2048,3072]{1,0:T(8,128)(2,1)S(1)}, u32[]{:S(2)}) %copy-start.1) | copy-done | bytes 12582936
  58.3 1.8 %all-to-all-done.1.came_ref = bf16[128,24,256]{2,1,0:T(8,128)(2,1)S(1)} async-done(((bf16[128,24,256]{2,1,0:T(8,128)(2,1)}), bf16[128,24,256]{2,1,0:T(8,128)(2,1)S(1)}, u32[]{:S(2)}, u32[]{:S(2)}) %all-to-all-start.1) | async-done | bytes 1572896 | tf_op jit(solution)/shard_map/all_to_all | solution.py:197
  60.1 0.0 copy-done.3
  60.1 0.0 copy-start.2
  60.1 4.6 %copy-done.2 = bf16[2048,3072]{1,0:T(8,128)(2,1)S(1)} copy-done((bf16[2048,3072]{1,0:T(8,128)(2,1)S(1)}, bf16[2048,3072]{1,0:T(8,128)(2,1)}, u32[]{:S(2)}) %copy-start.2) | copy-done | bytes 12582936
  64.7 5.5 %combine.1 = bf16[2048,256]{1,0:T(8,128)(2,1)} custom-call(bf16[2048,3072]{1,0:T(8,128)(2,1)S(1)} %copy-done.2, bf16[128,24,256]{2,1,0:T(8,128)(2,1)S(1)} %all-to-all-done.1.came_ref, bf16[256,256]{1,0:T(8,128)(2,1)S(1)} %copy-done.3), custom_call_target="tpu_custom_call" | custom-call | flops 3221225472 | bytes 16777216 | tf_op jit(solution)/shard_map/combine/pallas_call | solution.py:154
Async XLA Ops:
  0.0 13.1 %copy-start = (bf16[768,256]{1,0:T(8,128)(2,1)S(1)}, bf16[768,256]{1,0:T(8,128)(2,1)}, u32[]{:S(2)}) copy-start(bf16[768,256]{1,0:T(8,128)(2,1)} %param.22) | copy-start | bytes 1179652
  0.0 16.3 %copy-start.6 = (f32[1024,256]{1,0:T(8,128)S(1)}, f32[1024,256]{1,0:T(8,128)}, u32[]{:S(2)}) copy-start(f32[1024,256]{1,0:T(8,128)} %param.13) | copy-start | bytes 3145732
  1.6 21.1 %all-to-all-start = ((s32[128,1,128]{2,1,0:T(1,128)}), s32[128,1,128]{2,1,0:T(1,128)S(1)}, u32[]{:S(2)}, u32[]{:S(2)}) async-start(s32[128,1,128]{2,1,0:T(1,128)} %bitcast.11), calls=%async_computation | async-start | bytes 131072 | tf_op jit(solution)/shard_map/all_to_all | solution.py:191
  22.7 0.6 copy-start.7
  23.3 12.6 %copy-start.4 = (s32[512]{0:T(512)S(1)}, s32[512]{0:T(512)}, u32[]{:S(2)}) copy-start(s32[512]{0:T(512)} %rows_ref.1) | copy-start | bytes 6148
  23.3 12.6 %copy-start.5 = (s32[512]{0:T(512)S(1)}, s32[512]{0:T(512)}, u32[]{:S(2)}) copy-start(s32[512]{0:T(512)} %cols_ref.1) | copy-start | bytes 6148
  30.7 29.4 %all-to-all-start.1 = ((bf16[128,24,256]{2,1,0:T(8,128)(2,1)}), bf16[128,24,256]{2,1,0:T(8,128)(2,1)S(1)}, u32[]{:S(2)}, u32[]{:S(2)}) async-start(bf16[128,24,256]{2,1,0:T(8,128)(2,1)} %pick_rows.1), calls=%async_computation.1 | async-start | bytes 3145728 | tf_op jit(solution)/shard_map/all_to_all | solution.py:197
  35.9 24.3 %copy-start.3 = (bf16[256,256]{1,0:T(8,128)(2,1)S(1)}, bf16[256,256]{1,0:T(8,128)(2,1)}, u32[]{:S(2)}) copy-start(bf16[256,256]{1,0:T(8,128)(2,1)} %w_ref.1) | copy-start | bytes 393220
  53.8 4.5 %copy-start.1 = (bf16[2048,3072]{1,0:T(8,128)(2,1)}, bf16[2048,3072]{1,0:T(8,128)(2,1)S(1)}, u32[]{:S(2)}) copy-start(bf16[2048,3072]{1,0:T(8,128)(2,1)S(1)} %build_dense.1.dense_ref) | copy-start | bytes 37748740
  60.1 4.6 %copy-start.2 = (bf16[2048,3072]{1,0:T(8,128)(2,1)S(1)}, bf16[2048,3072]{1,0:T(8,128)(2,1)}, u32[]{:S(2)}) copy-start(bf16[2048,3072]{1,0:T(8,128)(2,1)} %copy-done.1) | copy-start | bytes 37748740

commit v2 on v1

v2 whole, which is shorter than its diff:
```python
import functools

import jax
import jax.numpy as jnp
from jax import lax
from jax.experimental import pallas as pl
from jax.experimental.pallas import tpu as pltpu
from jax.sharding import PartitionSpec as P

LANES = 128
TILE_CHUNKS = 8
TILE_UNROLL = 4
OUT_SLOTS = 8
PICK_PARTS = 2
ROWS_STEP = 512
PROJECT_STEP = 256


def pack_kernel(req_ref, halo_ref, req_count_ref, halo_count_ref, out_ref):
    req = req_ref[...]
    halo = halo_ref[...]
    req_slot = lax.broadcasted_iota(jnp.int32, req.shape, 0)
    halo_slot = lax.broadcasted_iota(jnp.int32, halo.shape, 0)
    req = jnp.where(req_slot < req_count_ref[...], req, -1)
    halo = jnp.where(halo_slot < halo_count_ref[...], halo, -1)
    rest = jnp.full((LANES - req.shape[0] - halo.shape[0], req.shape[1]), -1, jnp.int32)
    out_ref[...] = jnp.concatenate([req, halo, rest], axis=0).T


def pack_ids(req_t, halo_t, req_count, halo_count):
    owners = req_t.shape[1]
    return pl.pallas_call(
        pack_kernel,
        out_shape=jax.ShapeDtypeStruct((owners, LANES), jnp.int32),
        name="pack_ids",
    )(req_t, halo_t, req_count, halo_count)


def project_kernel(
    features_ref, history_ref, w_ref, proj_ref, hist_ref, rows_ref, old_ref, row_sem, old_sem
):
    step = PROJECT_STEP
    steps = proj_ref.shape[0] // step

    def fetch(k):
        at = pl.ds(k * step, step)
        return pltpu.make_async_copy(features_ref.at[at], rows_ref.at[at], row_sem.at[k])

    old = pltpu.make_async_copy(history_ref, old_ref, old_sem)
    for k in range(steps):
        fetch(k).start()
    old.start()

    @pl.loop(0, steps)
    def _(k):
        fetch(k).wait()
        at = pl.ds(pl.multiple_of(k * step, step), step)
        proj_ref[at] = jnp.dot(
            rows_ref[at].astype(jnp.bfloat16), w_ref[...], preferred_element_type=jnp.float32
        ).astype(jnp.bfloat16)

    old.wait()
    hist_ref[...] = old_ref[...].astype(jnp.bfloat16)


def project(features, history, w_in):
    rows, width = features.shape
    hidden = w_in.shape[1]
    table = jax.ShapeDtypeStruct((rows, hidden), jnp.bfloat16)
    vmem = pl.BlockSpec(memory_space=pltpu.VMEM)
    hbm = pl.BlockSpec(memory_space=pltpu.HBM)
    return pl.pallas_call(
        project_kernel,
        in_specs=[hbm, hbm, vmem],
        out_specs=[vmem, vmem],
        out_shape=[table, table],
        scratch_shapes=[
            pltpu.VMEM((rows, width), jnp.float32),
            pltpu.VMEM((rows, hidden), jnp.float32),
            pltpu.SemaphoreType.DMA((rows // PROJECT_STEP,)),
            pltpu.SemaphoreType.DMA,
        ],
        cost_estimate=pl.CostEstimate(
            flops=2 * rows * width * hidden, bytes_accessed=5 << 20, transcendentals=0
        ),
        compiler_params=pltpu.CompilerParams(vmem_limit_bytes=60 << 20),
        name="project",
    )(features, history, w_in)


def pick_kernel(req, halo, ids_ref, proj_ref, hist_ref, out_ref, req_ref, halo_ref, sem):
    count = ids_ref.shape[0]
    rows = proj_ref.shape[0]
    turned = ids_ref[...].T

    def pick(table_ref, start, size, first, last):
        wide = jnp.concatenate(
            [
                jnp.broadcast_to(turned[start : start + size, c : c + 1], (size, LANES))
                for c in range(first, last)
            ],
            axis=0,
        )
        high = (wide >> 7).astype(jnp.float32).astype(jnp.bfloat16)
        low = (wide & (LANES - 1)).astype(jnp.float32).astype(jnp.bfloat16)
        lane = lax.broadcasted_iota(jnp.int32, wide.shape, 1)
        lane = lane.astype(jnp.float32).astype(jnp.bfloat16)
        one, zero = jnp.ones_like(low), jnp.zeros_like(low)
        hit = jnp.where(low == lane, one, zero)
        parts = [
            jnp.where(high == jnp.full_like(high, k), hit, zero) for k in range(rows // LANES)
        ]
        picked = jnp.dot(
            jnp.concatenate(parts, axis=1), table_ref[...], preferred_element_type=jnp.float32
        )
        return picked.astype(jnp.bfloat16).reshape(last - first, size, -1)

    copies = []

    def send(held_ref, start, size, first, last):
        copy = pltpu.make_async_copy(
            held_ref.at[first:last],
            out_ref.at[first:last, start : start + size, :],
            sem.at[len(copies)],
        )
        copy.start()
        copies.append(copy)

    halo_ref[...] = pick(hist_ref, req, halo, 0, count)
    send(halo_ref, req, halo, 0, count)
    part = count // PICK_PARTS
    for first in range(0, count, part):
        req_ref[first : first + part] = pick(proj_ref, 0, req, first, first + part)
        send(req_ref, 0, req, first, first + part)
    for copy in copies:
        copy.wait()


def pick_rows(ids, proj, hist, req, halo):
    count = ids.shape[0]
    hidden = proj.shape[1]
    flops = 2 * count * (req + halo) * proj.shape[0] * hidden
    vmem = pl.BlockSpec(memory_space=pltpu.VMEM)
    return pl.pallas_call(
        functools.partial(pick_kernel, req, halo),
        in_specs=[vmem, vmem, vmem],
        out_specs=pl.BlockSpec(memory_space=pltpu.HBM),
        out_shape=jax.ShapeDtypeStruct((count, req + halo, hidden), jnp.bfloat16),
        scratch_shapes=[
            pltpu.VMEM((count, req, hidden), jnp.bfloat16),
            pltpu.VMEM((count, halo, hidden), jnp.bfloat16),
            pltpu.SemaphoreType.DMA((1 + PICK_PARTS,)),
        ],
        cost_estimate=pl.CostEstimate(flops=flops, bytes_accessed=3 << 20, transcendentals=0),
        compiler_params=pltpu.CompilerParams(vmem_limit_bytes=24 << 20),
        name="pick_rows",
    )(ids, proj, hist)


def dense_kernel(
    rows_ref, cols_ref, used_ref, tiles_ref, out_ref,
    held_ref, acc_ref, stage_ref, in_sem, out_sem,
):
    slots, side, _ = tiles_ref.shape
    blocks = acc_ref.shape[0] - 1
    row_blocks, width = out_ref.shape[0] // side, out_ref.shape[1]
    col_blocks = width // side
    chunk = slots // TILE_CHUNKS

    def fetch(c):
        at = pl.ds(c * chunk, chunk)
        return pltpu.make_async_copy(tiles_ref.at[at], held_ref.at[at], in_sem.at[c])

    def flush(r, slot):
        return pltpu.make_async_copy(
            stage_ref.at[slot], out_ref.at[pl.ds(r * side, side)], out_sem.at[slot]
        )

    for c in range(TILE_CHUNKS):
        fetch(c).start()

    @pl.loop(0, blocks)
    def _(b):
        acc_ref[b] = jnp.zeros(acc_ref.shape[1:], jnp.float32)

    @pl.loop(0, TILE_CHUNKS)
    def _(c):
        fetch(c).wait()

        live = jnp.clip(used_ref[0] - c * chunk, 0, chunk)

        @pl.loop(0, (live + TILE_UNROLL - 1) // TILE_UNROLL)
        def _(g):
            for u in range(TILE_UNROLL):
                t = c * chunk + g * TILE_UNROLL + u
                block = rows_ref[t] * col_blocks + cols_ref[t]
                block = jnp.where(t < used_ref[0], block, blocks)
                acc_ref[block] = acc_ref[block] + held_ref[t].astype(jnp.float32)

    @pl.loop(0, row_blocks)
    def _(r):
        slot = lax.rem(r, OUT_SLOTS)

        @pl.when(r >= OUT_SLOTS)
        def _():
            flush(r - OUT_SLOTS, slot).wait()

        for k in range(col_blocks):
            stage_ref[slot, :, k * side : (k + 1) * side] = acc_ref[r * col_blocks + k].astype(
                jnp.bfloat16
            )
        flush(r, slot).start()

    for r in range(row_blocks - OUT_SLOTS, row_blocks):
        flush(r, r % OUT_SLOTS).wait()


def build_dense(tile_rows, tile_cols, tile_count, tile_values, row_blocks, col_blocks):
    slots, side, _ = tile_values.shape
    smem = pl.BlockSpec(memory_space=pltpu.SMEM)
    hbm = pl.BlockSpec(memory_space=pltpu.HBM)
    return pl.pallas_call(
        dense_kernel,
        in_specs=[smem, smem, smem, hbm],
        out_specs=hbm,
        out_shape=jax.ShapeDtypeStruct((row_blocks * side, col_blocks * side), jnp.bfloat16),
        scratch_shapes=[
            pltpu.VMEM((slots, side, side), jnp.bfloat16),
            pltpu.VMEM((row_blocks * col_blocks + 1, side, side), jnp.float32),
            pltpu.VMEM((OUT_SLOTS, side, col_blocks * side), jnp.bfloat16),
            pltpu.SemaphoreType.DMA((TILE_CHUNKS,)),
            pltpu.SemaphoreType.DMA((OUT_SLOTS,)),
        ],
        compiler_params=pltpu.CompilerParams(vmem_limit_bytes=56 << 20),
        cost_estimate=pl.CostEstimate(flops=1 << 20, bytes_accessed=30 << 20, transcendentals=0),
        name="build_dense",
    )(tile_rows, tile_cols, tile_count, tile_values)


def combine_kernel(
    req, dense_ref, came_ref, w_ref, out_ref, held_ref, source_ref, stage_ref, in_sem, out_sem
):
    owners, slots, hidden = came_ref.shape
    nodes = owners * req
    step = ROWS_STEP
    steps = nodes // step

    def fetch(k):
        at = pl.ds(k * step, step)
        return pltpu.make_async_copy(dense_ref.at[at], held_ref.at[at], in_sem.at[k])

    def flush(k):
        at = pl.ds(k * step, step)
        return pltpu.make_async_copy(stage_ref.at[at], out_ref.at[at], out_sem.at[k])

    for k in range(2):
        fetch(k).start()
    source_ref[:nodes] = came_ref[:, :req, :].reshape(nodes, hidden)
    source_ref[nodes:] = came_ref[:, req:, :].reshape(owners * (slots - req), hidden)

    @pl.loop(0, steps)
    def _(k):
        fetch(k).wait()

        @pl.when(k + 2 < steps)
        def _():
            fetch(k + 2).start()

        at = pl.ds(pl.multiple_of(k * step, step), step)
        total = jnp.dot(held_ref[at], source_ref[...], preferred_element_type=jnp.float32)
        mixed = jnp.dot(total.astype(jnp.bfloat16), w_ref[...], preferred_element_type=jnp.float32)
        own = source_ref[at].astype(jnp.float32)
        stage_ref[at] = jnp.maximum(mixed + own, 0.0).astype(jnp.bfloat16)
        flush(k).start()

    for k in range(steps):
        flush(k).wait()


def combine(dense, came, w_out, req):
    hidden = came.shape[2]
    nodes, width = dense.shape
    vmem = pl.BlockSpec(memory_space=pltpu.VMEM)
    hbm = pl.BlockSpec(memory_space=pltpu.HBM)
    return pl.pallas_call(
        functools.partial(combine_kernel, req),
        in_specs=[hbm, vmem, vmem],
        out_specs=hbm,
        out_shape=jax.ShapeDtypeStruct((nodes, hidden), jnp.bfloat16),
        scratch_shapes=[
            pltpu.VMEM((nodes, width), jnp.bfloat16),
            pltpu.VMEM((width, hidden), jnp.bfloat16),
            pltpu.VMEM((nodes, hidden), jnp.bfloat16),
            pltpu.SemaphoreType.DMA((nodes // ROWS_STEP,)),
            pltpu.SemaphoreType.DMA((nodes // ROWS_STEP,)),
        ],
        cost_estimate=pl.CostEstimate(
            flops=2 * nodes * width * hidden, bytes_accessed=16 << 20, transcendentals=0
        ),
        compiler_params=pltpu.CompilerParams(vmem_limit_bytes=52 << 20),
        name="combine",
    )(dense, came, w_out)


def on_device(
    features,
    history,
    request_ids,
    request_count,
    halo_ids,
    halo_count,
    tile_values,
    tile_rows,
    tile_cols,
    tile_count,
    w_in,
    w_out,
):
    owners, req = request_ids.shape[1:]
    halo = halo_ids.shape[2]
    side = tile_values.shape[1]
    wanted = pack_ids(request_ids[0].T, halo_ids[0].T, request_count, halo_count)
    asked = lax.all_to_all(wanted, "nodes", split_axis=0, concat_axis=0, tiled=True)
    proj, hist = project(features, history, w_in)
    picked = pick_rows(asked, proj, hist, req, halo)
    picked, tile_count = lax.optimization_barrier((picked, tile_count))
    came = lax.all_to_all(picked, "nodes", split_axis=0, concat_axis=0, tiled=True)
    dense = build_dense(
        tile_rows, tile_cols, tile_count, tile_values,
        owners * req // side, owners * (req + halo) // side,
    )
    return combine(dense, came, w_out, req)


def solution(mesh):
    in_specs = (
        P("nodes", None),
        P("nodes", None),
        P("nodes", None, None),
        P("nodes", None),
        P("nodes", None, None),
        P("nodes", None),
        P("nodes", None, None),
        P("nodes"),
        P("nodes"),
        P("nodes"),
        P(),
        P(),
    )
    out_specs = P("nodes", None)
    return jax.shard_map(
        on_device, mesh=mesh, in_specs=in_specs, out_specs=out_specs, check_vma=False
    )
```

time: 70.8 us -> 64.8 us (0.915)
  waiting for transfers between devices: 7.33 us -> 18.1 us
  local copies, waits for them, and re-layouts: 9.73 us -> 2.09 us
  Pallas kernels: 32.4 us -> 27.5 us
  matrix products: 3.26 us -> 0 us
  other arithmetic: 0.84 us -> 0 us
    all_to_all x1, waiting for transfers between devices: 1.84 us -> 12.7 us  [on_device(): lax.all_to_all(picked, 'nodes', split_axis=0, concat_axis=0, tiled=True)]
    unnamed x16 -> x6, local copies, waits for them, and re-layouts: 9.73 us -> 2.09 us
    pallas_call x3 -> x4, Pallas kernels: 30.8 us -> 26.1 us  [the longest x1 11.5 us: build_dense(): pl.pallas_call(dense_kernel, in_specs=[smem, smem, smem, hbm], out_specs=...]
    dot_general x1 -> x0, matrix products: 3.26 us -> none  [on_device(): jnp.dot(features.astype(jnp.bfloat16), w_in, preferred_element_type=jnp.f...]
    convert_element_type x1 -> x0, other arithmetic: 0.84 us -> none  [on_device(): picked = pick_rows(asked, proj, history.astype(jnp.bfloat16), req, halo)]
  transfers between devices with their start and end apart: 2 -> 2, of which waited for: 2 -> 2; matrix products, arithmetic and copies ran while one was open for 6% -> 0% of each run, Pallas kernels for 25% -> 24%
where the time goes in v2:
time: 64.8 us; the launch traced here: 64.4 us
  Pallas kernels  27.5 us (42%)
  waiting for transfers between devices  18.1 us (28%)
  starting transfers between devices  16 us (25%)
  local copies, waits for them, and re-layouts  2.09 us (3%)
  between operations  0.7 us (1%)
    all_to_all x1, waiting for transfers between devices, on_device(): lax.all_to_all(picked, 'nodes', split_axis=0, concat_axis=0, tiled=True)  12.7 us
    pallas_call x1, Pallas kernels, build_dense(): pl.pallas_call(dense_kernel, in_specs=[smem, smem, smem, hbm], out_specs=...  11.5 us
    all_to_all x1, starting transfers between devices, on_device(): lax.all_to_all(wanted, 'nodes', split_axis=0, concat_axis=0, tiled=True)  11.5 us
    pallas_call x1, Pallas kernels, combine(): pl.pallas_call(functools.partial(combine_kernel, req), in_specs=[hbm, vme...  7.35 us
    all_to_all x1, waiting for transfers between devices, on_device(): lax.all_to_all(wanted, 'nodes', split_axis=0, concat_axis=0, tiled=True)  5.37 us
    all_to_all x1, starting transfers between devices, on_device(): lax.all_to_all(picked, 'nodes', split_axis=0, concat_axis=0, tiled=True)  4.49 us
    pallas_call x1, Pallas kernels, project(): pl.pallas_call(project_kernel, in_specs=[hbm, hbm, vmem], out_specs=[vmem...  4.23 us
    pallas_call x1, Pallas kernels, pick_rows(): pl.pallas_call(functools.partial(pick_kernel, req, halo), in_specs=[vmem,...  2.98 us
  transfers between devices with their start and end apart: 2, of which 2 were waited for; matrix products, arithmetic and copies ran while one was open for 0% of the time, Pallas kernels for 24%

profile of v2, /device:TPU:1, one launch (start us, length us, event | category | flops | bytes accessed | tf_op | source)
XLA Modules:
  0.0 64.4 jit_solution(17052106175041554255)
XLA Ops:
  0.0 1.4 %pack_ids.1 = s32[128,128]{1,0:T(8,128)} custom-call(s32[16,128]{1,0:T(8,128)} %bitcast.12, s32[8,128]{1,0:T(8,128)} %bitcast.13, s32[1,128]{1,0:T(1,128)} %req_count_ref.1, s32[1,128]{1,0:T(1,128)} %halo_count_ref.1), custom_call_target="tpu_custom_call" | custom-call | tf_op jit(solution)/shard_map/pack_ids/pallas_call | solution.py:32
  1.4 11.5 %all-to-all-start = ((s32[128,1,128]{2,1,0:T(1,128)}), s32[128,1,128]{2,1,0:T(1,128)S(1)}, u32[]{:S(2)}, u32[]{:S(2)}) async-start(s32[128,1,128]{2,1,0:T(1,128)} %bitcast.11), calls=%async_computation | async-start | bytes 131072 | tf_op jit(solution)/shard_map/all_to_all | solution.py:323
  12.9 4.2 %project.1 = (bf16[1024,256]{1,0:T(8,128)(2,1)}, bf16[1024,256]{1,0:T(8,128)(2,1)}) custom-call(f32[1024,768]{1,0:T(8,128)} %features_ref.1, f32[1024,256]{1,0:T(8,128)} %history_ref.1, bf16[768,256]{1,0:T(8,128)(2,1)} %w_ref.2), custom_call_target="tpu_custom_call" | custom-call | flops 402653184 | bytes 5242880 | tf_op jit(solution)/shard_map/project/pallas_call | solution.py:72
  17.2 5.4 %all-to-all-done = s32[128,1,128]{2,1,0:T(1,128)S(1)} async-done(((s32[128,1,128]{2,1,0:T(1,128)}), s32[128,1,128]{2,1,0:T(1,128)S(1)}, u32[]{:S(2)}, u32[]{:S(2)}) %all-to-all-start) | async-done | bytes 65568 | tf_op jit(solution)/shard_map/all_to_all | solution.py:323
  22.6 0.0 copy-start.1
  22.6 1.0 %copy-done.1 = bf16[1024,256]{1,0:T(8,128)(2,1)S(1)} copy-done((bf16[1024,256]{1,0:T(8,128)(2,1)S(1)}, bf16[1024,256]{1,0:T(8,128)(2,1)}, u32[]{:S(2)}) %copy-start.1) | copy-done | bytes 524312
  23.6 0.0 copy-start.2
  23.6 1.0 %copy-done.2 = bf16[1024,256]{1,0:T(8,128)(2,1)S(1)} copy-done((bf16[1024,256]{1,0:T(8,128)(2,1)S(1)}, bf16[1024,256]{1,0:T(8,128)(2,1)}, u32[]{:S(2)}) %copy-start.2) | copy-done | bytes 524312
  24.6 3.0 %pick_rows.1 = bf16[128,24,256]{2,1,0:T(8,128)(2,1)} custom-call(s32[128,128]{1,0:T(8,128)S(1)} %bitcast.10, bf16[1024,256]{1,0:T(8,128)(2,1)S(1)} %copy-done.1, bf16[1024,256]{1,0:T(8,128)(2,1)S(1)} %copy-done.2), custom_call_target="tpu_custom_call" | custom-call | flops 1610612736 | bytes 3145728 | tf_op jit(solution)/shard_map/pick_rows/pallas_call | solution.py:144
  27.6 4.5 %all-to-all-start.1 = ((bf16[128,24,256]{2,1,0:T(8,128)(2,1)}), bf16[128,24,256]{2,1,0:T(8,128)(2,1)S(1)}, u32[]{:S(2)}, u32[]{:S(2)}) async-start(bf16[128,24,256]{2,1,0:T(8,128)(2,1)} %pick_rows.1), calls=%async_computation.1 | async-start | bytes 3145728 | tf_op jit(solution)/shard_map/all_to_all | solution.py:327
  32.8 0.0 copy-start
  32.8 11.5 %build_dense.1.dense_ref = bf16[2048,3072]{1,0:T(8,128)(2,1)} custom-call(s32[512]{0:T(512)} %rows_ref.1, s32[512]{0:T(512)} %cols_ref.1, s32[1]{0:T(128)S(6)} %copy.14.used_ref, bf16[512,128,128]{2,1,0:T(8,128)(2,1)} %tiles_ref.1), custom_call_target="tpu_custom_call" | custom-call | flops 1048576 | bytes 31457280 | tf_op jit(solution)/shard_map/build_dense/pallas_call | solution.py:222
  44.3 12.7 %all-to-all-done.1.came_ref = bf16[128,24,256]{2,1,0:T(8,128)(2,1)S(1)} async-done(((bf16[128,24,256]{2,1,0:T(8,128)(2,1)}), bf16[128,24,256]{2,1,0:T(8,128)(2,1)S(1)}, u32[]{:S(2)}, u32[]{:S(2)}) %all-to-all-start.1) | async-done | bytes 1572896 | tf_op jit(solution)/shard_map/all_to_all | solution.py:327
  57.0 0.0 copy-done
  57.0 7.4 %combine.1 = bf16[2048,256]{1,0:T(8,128)(2,1)} custom-call(bf16[2048,3072]{1,0:T(8,128)(2,1)} %build_dense.1.dense_ref, bf16[128,24,256]{2,1,0:T(8,128)(2,1)S(1)} %all-to-all-done.1.came_ref, bf16[256,256]{1,0:T(8,128)(2,1)S(1)} %copy-done), custom_call_target="tpu_custom_call" | custom-call | flops 3221225472 | bytes 16777216 | tf_op jit(solution)/shard_map/combine/pallas_call | solution.py:285
Async XLA Ops:
  1.4 21.1 %all-to-all-start = ((s32[128,1,128]{2,1,0:T(1,128)}), s32[128,1,128]{2,1,0:T(1,128)S(1)}, u32[]{:S(2)}, u32[]{:S(2)}) async-start(s32[128,1,128]{2,1,0:T(1,128)} %bitcast.11), calls=%async_computation | async-start | bytes 131072 | tf_op jit(solution)/shard_map/all_to_all | solution.py:323
  22.6 1.0 %copy-start.1 = (bf16[1024,256]{1,0:T(8,128)(2,1)S(1)}, bf16[1024,256]{1,0:T(8,128)(2,1)}, u32[]{:S(2)}) copy-start(bf16[1024,256]{1,0:T(8,128)(2,1)} %get-tuple-element.9.proj_ref) | copy-start | bytes 1572868
  23.6 1.0 %copy-start.2 = (bf16[1024,256]{1,0:T(8,128)(2,1)S(1)}, bf16[1024,256]{1,0:T(8,128)(2,1)}, u32[]{:S(2)}) copy-start(bf16[1024,256]{1,0:T(8,128)(2,1)} %get-tuple-element.10.hist_ref) | copy-start | bytes 1572868
  27.6 29.4 %all-to-all-start.1 = ((bf16[128,24,256]{2,1,0:T(8,128)(2,1)}), bf16[128,24,256]{2,1,0:T(8,128)(2,1)S(1)}, u32[]{:S(2)}, u32[]{:S(2)}) async-start(bf16[128,24,256]{2,1,0:T(8,128)(2,1)} %pick_rows.1), calls=%async_computation.1 | async-start | bytes 3145728 | tf_op jit(solution)/shard_map/all_to_all | solution.py:327
  32.8 24.3 %copy-start = (bf16[256,256]{1,0:T(8,128)(2,1)S(1)}, bf16[256,256]{1,0:T(8,128)(2,1)}, u32[]{:S(2)}) copy-start(bf16[256,256]{1,0:T(8,128)(2,1)} %w_ref.3) | copy-start | bytes 393220

commit v3 on v2

--- a/solution.py
+++ b/solution.py
@@ -13,7 +13,8 @@
 OUT_SLOTS = 8
 PICK_PARTS = 2
 ROWS_STEP = 512
-PROJECT_STEP = 256
+KEPT_ROWS = 256
+PROJECT_STEP = 512
 
 
 def pack_kernel(req_ref, halo_ref, req_count_ref, halo_count_ref, out_ref):
@@ -31,7 +32,8 @@
     owners = req_t.shape[1]
     return pl.pallas_call(
         pack_kernel,
-        out_shape=jax.ShapeDtypeStruct((owners, LANES), jnp.int32),
+        out_specs=pl.BlockSpec(memory_space=pltpu.VMEM),
+        out_shape=pltpu.VMEM((owners, LANES), jnp.int32),
         name="pack_ids",
     )(req_t, halo_t, req_count, halo_count)
 
@@ -66,7 +68,9 @@
 def project(features, history, w_in):
     rows, width = features.shape
     hidden = w_in.shape[1]
-    table = jax.ShapeDtypeStruct((rows, hidden), jnp.bfloat16)
+    table = pltpu.VMEM((rows, hidden), jnp.bfloat16)
+    features = pltpu.with_memory_space_constraint(features, pltpu.HBM)
+    history = pltpu.with_memory_space_constraint(history, pltpu.HBM)
     vmem = pl.BlockSpec(memory_space=pltpu.VMEM)
     hbm = pl.BlockSpec(memory_space=pltpu.HBM)
     return pl.pallas_call(
@@ -158,11 +162,12 @@
 
 
 def dense_kernel(
-    rows_ref, cols_ref, used_ref, tiles_ref, out_ref,
+    rows_ref, cols_ref, used_ref, tiles_ref, kept_ref, out_ref,
     held_ref, acc_ref, stage_ref, in_sem, out_sem,
 ):
     slots, side, _ = tiles_ref.shape
     blocks = acc_ref.shape[0] - 1
+    kept_blocks = kept_ref.shape[0] // side
     row_blocks, width = out_ref.shape[0] // side, out_ref.shape[1]
     col_blocks = width // side
     chunk = slots // TILE_CHUNKS
@@ -206,10 +211,18 @@
             flush(r - OUT_SLOTS, slot).wait()
 
         for k in range(col_blocks):
-            stage_ref[slot, :, k * side : (k + 1) * side] = acc_ref[r * col_blocks + k].astype(
+            stage_ref[slot, :, k * side : (k + 1) * side] = acc_ref[
+                (kept_blocks + r) * col_blocks + k
+            ].astype(jnp.bfloat16)
+        flush(r, slot).start()
+
+    @pl.loop(0, kept_blocks)
+    def _(r):
+        at = pl.ds(pl.multiple_of(r * side, side), side)
+        for k in range(col_blocks):
+            kept_ref[at, k * side : (k + 1) * side] = acc_ref[r * col_blocks + k].astype(
                 jnp.bfloat16
             )
-        flush(r, slot).start()
 
     for r in range(row_blocks - OUT_SLOTS, row_blocks):
         flush(r, r % OUT_SLOTS).wait()
@@ -217,13 +230,18 @@
 
 def build_dense(tile_rows, tile_cols, tile_count, tile_values, row_blocks, col_blocks):
     slots, side, _ = tile_values.shape
+    width = col_blocks * side
+    tile_values = pltpu.with_memory_space_constraint(tile_values, pltpu.HBM)
     smem = pl.BlockSpec(memory_space=pltpu.SMEM)
     hbm = pl.BlockSpec(memory_space=pltpu.HBM)
     return pl.pallas_call(
         dense_kernel,
         in_specs=[smem, smem, smem, hbm],
-        out_specs=hbm,
-        out_shape=jax.ShapeDtypeStruct((row_blocks * side, col_blocks * side), jnp.bfloat16),
+        out_specs=[pl.BlockSpec(memory_space=pltpu.VMEM), hbm],
+        out_shape=[
+            pltpu.VMEM((KEPT_ROWS, width), jnp.bfloat16),
+            jax.ShapeDtypeStruct((row_blocks * side - KEPT_ROWS, width), jnp.bfloat16),
+        ],
         scratch_shapes=[
             pltpu.VMEM((slots, side, side), jnp.bfloat16),
             pltpu.VMEM((row_blocks * col_blocks + 1, side, side), jnp.float32),
@@ -238,33 +256,51 @@
 
 
 def combine_kernel(
-    req, dense_ref, came_ref, w_ref, out_ref, held_ref, source_ref, stage_ref, in_sem, out_sem
+    req, kept_ref, dense_ref, came_ref, w_ref, out_ref,
+    held_ref, source_ref, stage_ref, kept_sem, in_sem, out_sem,
 ):
     owners, slots, hidden = came_ref.shape
     nodes = owners * req
     step = ROWS_STEP
     steps = nodes // step
 
-    def fetch(k):
-        at = pl.ds(k * step, step)
-        return pltpu.make_async_copy(dense_ref.at[at], held_ref.at[at], in_sem.at[k])
+    kept = kept_ref.shape[0]
+
+    def fetch(first, size, k):
+        return pltpu.make_async_copy(
+            dense_ref.at[pl.ds(first - kept, size)], held_ref.at[pl.ds(first, size)], in_sem.at[k]
+        )
+
+    def fetch_step(k):
+        return fetch(k * step, step, k)
+
+    near = pltpu.make_async_copy(kept_ref, held_ref.at[pl.ds(0, kept)], kept_sem)
+    start = fetch(kept, step - kept, 0)
 
     def flush(k):
         at = pl.ds(k * step, step)
         return pltpu.make_async_copy(stage_ref.at[at], out_ref.at[at], out_sem.at[k])
 
-    for k in range(2):
-        fetch(k).start()
+    start.start()
+    near.start()
+    fetch_step(1).start()
     source_ref[:nodes] = came_ref[:, :req, :].reshape(nodes, hidden)
     source_ref[nodes:] = came_ref[:, req:, :].reshape(owners * (slots - req), hidden)
 
     @pl.loop(0, steps)
     def _(k):
-        fetch(k).wait()
+        @pl.when(k == 0)
+        def _():
+            start.wait()
+            near.wait()
+
+        @pl.when(k > 0)
+        def _():
+            fetch_step(k).wait()
 
         @pl.when(k + 2 < steps)
         def _():
-            fetch(k + 2).start()
+            fetch_step(k + 2).start()
 
         at = pl.ds(pl.multiple_of(k * step, step), step)
         total = jnp.dot(held_ref[at], source_ref[...], preferred_element_type=jnp.float32)
@@ -277,29 +313,31 @@
         flush(k).wait()
 
 
-def combine(dense, came, w_out, req):
+def combine(kept, dense, came, w_out, req):
     hidden = came.shape[2]
-    nodes, width = dense.shape
+    nodes, width = kept.shape[0] + dense.shape[0], dense.shape[1]
+    dense = pltpu.with_memory_space_constraint(dense, pltpu.HBM)
     vmem = pl.BlockSpec(memory_space=pltpu.VMEM)
     hbm = pl.BlockSpec(memory_space=pltpu.HBM)
     return pl.pallas_call(
         functools.partial(combine_kernel, req),
-        in_specs=[hbm, vmem, vmem],
+        in_specs=[vmem, hbm, vmem, vmem],
         out_specs=hbm,
         out_shape=jax.ShapeDtypeStruct((nodes, hidden), jnp.bfloat16),
         scratch_shapes=[
             pltpu.VMEM((nodes, width), jnp.bfloat16),
             pltpu.VMEM((width, hidden), jnp.bfloat16),
             pltpu.VMEM((nodes, hidden), jnp.bfloat16),
+            pltpu.SemaphoreType.DMA,
             pltpu.SemaphoreType.DMA((nodes // ROWS_STEP,)),
             pltpu.SemaphoreType.DMA((nodes // ROWS_STEP,)),
         ],
         cost_estimate=pl.CostEstimate(
             flops=2 * nodes * width * hidden, bytes_accessed=16 << 20, transcendentals=0
         ),
-        compiler_params=pltpu.CompilerParams(vmem_limit_bytes=52 << 20),
+        compiler_params=pltpu.CompilerParams(vmem_limit_bytes=24 << 20),
         name="combine",
-    )(dense, came, w_out)
+    )(kept, dense, came, w_out)
 
 
 def on_device(
@@ -325,11 +363,11 @@
     picked = pick_rows(asked, proj, hist, req, halo)
     picked, tile_count = lax.optimization_barrier((picked, tile_count))
     came = lax.all_to_all(picked, "nodes", split_axis=0, concat_axis=0, tiled=True)
-    dense = build_dense(
+    kept, dense = build_dense(
         tile_rows, tile_cols, tile_count, tile_values,
         owners * req // side, owners * (req + halo) // side,
     )
-    return combine(dense, came, w_out, req)
+    return combine(kept, dense, came, w_out, req)
 
 
 def solution(mesh):

time: 64.8 us -> 62.1 us (0.958)
  local copies, waits for them, and re-layouts: 2.09 us -> 0.01 us
  Pallas kernels: 27.5 us -> 26.1 us
  waiting for transfers between devices: 18.1 us -> 19 us
    unnamed x6 -> x2, local copies, waits for them, and re-layouts: 2.09 us -> 0.01 us
    pallas_call x1, Pallas kernels: 4.23 us -> 3.33 us  [project(): pl.pallas_call(project_kernel, in_specs=[hbm, hbm, vmem], out_specs=[vmem...]
    all_to_all x1, waiting for transfers between devices: 5.37 us -> 6.19 us  [on_device(): lax.all_to_all(wanted, 'nodes', split_axis=0, concat_axis=0, tiled=True)]
where the time goes in v3:
time: 62.1 us; the launch traced here: 61.8 us
  Pallas kernels  26.1 us (42%)
  waiting for transfers between devices  19 us (31%)
  starting transfers between devices  16 us (26%)
  between operations  0.7 us (1%)
    all_to_all x1, waiting for transfers between devices, on_device(): lax.all_to_all(picked, 'nodes', split_axis=0, concat_axis=0, tiled=True)  12.8 us
    all_to_all x1, starting transfers between devices, on_device(): lax.all_to_all(wanted, 'nodes', split_axis=0, concat_axis=0, tiled=True)  11.5 us
    pallas_call x1, Pallas kernels, build_dense(): pl.pallas_call(dense_kernel, in_specs=[smem, smem, smem, hbm], out_specs=...  11.4 us
    pallas_call x1, Pallas kernels, combine(): pl.pallas_call(functools.partial(combine_kernel, req), in_specs=[vmem, hb...  6.88 us
    all_to_all x1, waiting for transfers between devices, on_device(): lax.all_to_all(wanted, 'nodes', split_axis=0, concat_axis=0, tiled=True)  6.19 us
    all_to_all x1, starting transfers between devices, on_device(): lax.all_to_all(picked, 'nodes', split_axis=0, concat_axis=0, tiled=True)  4.51 us
    pallas_call x1, Pallas kernels, project(): pl.pallas_call(project_kernel, in_specs=[hbm, hbm, vmem], out_specs=[vmem...  3.33 us
    pallas_call x1, Pallas kernels, pick_rows(): pl.pallas_call(functools.partial(pick_kernel, req, halo), in_specs=[vmem,...  2.96 us
  transfers between devices with their start and end apart: 2, of which 2 were waited for; matrix products, arithmetic and copies ran while one was open for 0% of the time, Pallas kernels for 24%

profile of v3, /device:TPU:1, one launch (start us, length us, event | category | flops | bytes accessed | tf_op | source)
XLA Modules:
  0.0 61.8 jit_solution(9406932500033012329)
XLA Ops:
  0.0 1.4 %pack_ids.1 = s32[128,128]{1,0:T(8,128)} custom-call(s32[16,128]{1,0:T(8,128)} %bitcast.11, s32[8,128]{1,0:T(8,128)} %bitcast.12, s32[1,128]{1,0:T(1,128)} %req_count_ref.1, s32[1,128]{1,0:T(1,128)} %halo_count_ref.1), custom_call_target="tpu_custom_call" | custom-call | tf_op jit(solution)/shard_map/pack_ids/pallas_call | solution.py:33
  1.4 11.5 %all-to-all-start = ((s32[128,1,128]{2,1,0:T(1,128)}), s32[128,1,128]{2,1,0:T(1,128)S(1)}, u32[]{:S(2)}, u32[]{:S(2)}) async-start(s32[128,1,128]{2,1,0:T(1,128)} %bitcast.5), calls=%async_computation | async-start | bytes 131072 | tf_op jit(solution)/shard_map/all_to_all | solution.py:361
  13.0 3.3 %project.1 = (bf16[1024,256]{1,0:T(8,128)(2,1)S(1)}, bf16[1024,256]{1,0:T(8,128)(2,1)S(1)}) custom-call(f32[1024,768]{1,0:T(8,128)} %features_ref.1, f32[1024,256]{1,0:T(8,128)} %history_ref.1, bf16[768,256]{1,0:T(8,128)(2,1)} %w_ref.2), custom_call_target="tpu_custom_call" | custom-call | flops 402653184 | bytes 5242880 | tf_op jit(solution)/shard_map/project/pallas_call | solution.py:76
  16.3 6.2 %all-to-all-done = s32[128,1,128]{2,1,0:T(1,128)S(1)} async-done(((s32[128,1,128]{2,1,0:T(1,128)}), s32[128,1,128]{2,1,0:T(1,128)S(1)}, u32[]{:S(2)}, u32[]{:S(2)}) %all-to-all-start) | async-done | bytes 65568 | tf_op jit(solution)/shard_map/all_to_all | solution.py:361
  22.5 3.0 %pick_rows.1 = bf16[128,24,256]{2,1,0:T(8,128)(2,1)} custom-call(s32[128,128]{1,0:T(8,128)S(1)} %bitcast.10, bf16[1024,256]{1,0:T(8,128)(2,1)S(1)} %get-tuple-element.11.proj_ref, bf16[1024,256]{1,0:T(8,128)(2,1)S(1)} %get-tuple-element.12.hist_ref), custom_call_target="tpu_custom_call" | custom-call | flops 1610612736 | bytes 3145728 | tf_op jit(solution)/shard_map/pick_rows/pallas_call | solution.py:148
  25.4 4.5 %all-to-all-start.1 = ((bf16[128,24,256]{2,1,0:T(8,128)(2,1)}), bf16[128,24,256]{2,1,0:T(8,128)(2,1)S(1)}, u32[]{:S(2)}, u32[]{:S(2)}) async-start(bf16[128,24,256]{2,1,0:T(8,128)(2,1)} %pick_rows.1), calls=%async_computation.1 | async-start | bytes 3145728 | tf_op jit(solution)/shard_map/all_to_all | solution.py:365
  30.6 0.0 copy-start
  30.6 11.4 %build_dense.1 = (bf16[256,3072]{1,0:T(8,128)(2,1)S(1)}, bf16[1792,3072]{1,0:T(8,128)(2,1)}) custom-call(s32[512]{0:T(512)} %rows_ref.1, s32[512]{0:T(512)} %cols_ref.1, s32[1]{0:T(128)S(6)} %copy.14.used_ref, bf16[512,128,128]{2,1,0:T(8,128)(2,1)} %tiles_ref.1), custom_call_target="tpu_custom_call" | custom-call | flops 1048576 | bytes 31457280 | tf_op jit(solution)/shard_map/build_dense/pallas_call | solution.py:237
  42.1 12.8 %all-to-all-done.1.came_ref = bf16[128,24,256]{2,1,0:T(8,128)(2,1)S(1)} async-done(((bf16[128,24,256]{2,1,0:T(8,128)(2,1)}), bf16[128,24,256]{2,1,0:T(8,128)(2,1)S(1)}, u32[]{:S(2)}, u32[]{:S(2)}) %all-to-all-start.1) | async-done | bytes 1572896 | tf_op jit(solution)/shard_map/all_to_all | solution.py:365
  54.9 0.0 copy-done
  54.9 6.9 %combine.1 = bf16[2048,256]{1,0:T(8,128)(2,1)} custom-call(bf16[256,3072]{1,0:T(8,128)(2,1)S(1)} %get-tuple-element.14.kept_ref, bf16[1792,3072]{1,0:T(8,128)(2,1)} %get-tuple-element.15.dense_ref, bf16[128,24,256]{2,1,0:T(8,128)(2,1)S(1)} %all-to-all-done.1.came_ref, bf16[256,256]{1,0:T(8,128)(2,1)S(1)} %copy-done), custom_call_target="tpu_custom_call" | custom-call | flops 3221225472 | bytes 16777216 | tf_op jit(solution)/shard_map/combine/pallas_call | solution.py:322
Async XLA Ops:
  1.4 21.0 %all-to-all-start = ((s32[128,1,128]{2,1,0:T(1,128)}), s32[128,1,128]{2,1,0:T(1,128)S(1)}, u32[]{:S(2)}, u32[]{:S(2)}) async-start(s32[128,1,128]{2,1,0:T(1,128)} %bitcast.5), calls=%async_computation | async-start | bytes 131072 | tf_op jit(solution)/shard_map/all_to_all | solution.py:361
  25.4 29.4 %all-to-all-start.1 = ((bf16[128,24,256]{2,1,0:T(8,128)(2,1)}), bf16[128,24,256]{2,1,0:T(8,128)(2,1)S(1)}, u32[]{:S(2)}, u32[]{:S(2)}) async-start(bf16[128,24,256]{2,1,0:T(8,128)(2,1)} %pick_rows.1), calls=%async_computation.1 | async-start | bytes 3145728 | tf_op jit(solution)/shard_map/all_to_all | solution.py:365
  30.6 24.3 %copy-start = (bf16[256,256]{1,0:T(8,128)(2,1)S(1)}, bf16[256,256]{1,0:T(8,128)(2,1)}, u32[]{:S(2)}) copy-start(bf16[256,256]{1,0:T(8,128)(2,1)} %w_ref.3) | copy-start | bytes 393220

commit v4 on v3

--- a/solution.py
+++ b/solution.py
@@ -39,7 +39,8 @@
 
 
 def project_kernel(
-    features_ref, history_ref, w_ref, proj_ref, hist_ref, rows_ref, old_ref, row_sem, old_sem
+    features_ref, history_ref, w_in_ref, proj_ref, hist_ref,
+    rows_ref, old_ref, w_ref, row_sem, old_sem, w_sem,
 ):
     step = PROJECT_STEP
     steps = proj_ref.shape[0] // step
@@ -49,9 +50,14 @@
         return pltpu.make_async_copy(features_ref.at[at], rows_ref.at[at], row_sem.at[k])
 
     old = pltpu.make_async_copy(history_ref, old_ref, old_sem)
+    weights = pltpu.make_async_copy(w_in_ref, w_ref, w_sem)
+    old.start()
+    weights.start()
     for k in range(steps):
         fetch(k).start()
-    old.start()
+    old.wait()
+    hist_ref[...] = old_ref[...].astype(jnp.bfloat16)
+    weights.wait()
 
     @pl.loop(0, steps)
     def _(k):
@@ -61,9 +67,6 @@
             rows_ref[at].astype(jnp.bfloat16), w_ref[...], preferred_element_type=jnp.float32
         ).astype(jnp.bfloat16)
 
-    old.wait()
-    hist_ref[...] = old_ref[...].astype(jnp.bfloat16)
-
 
 def project(features, history, w_in):
     rows, width = features.shape
@@ -71,17 +74,20 @@
     table = pltpu.VMEM((rows, hidden), jnp.bfloat16)
     features = pltpu.with_memory_space_constraint(features, pltpu.HBM)
     history = pltpu.with_memory_space_constraint(history, pltpu.HBM)
+    w_in = pltpu.with_memory_space_constraint(w_in, pltpu.HBM)
     vmem = pl.BlockSpec(memory_space=pltpu.VMEM)
     hbm = pl.BlockSpec(memory_space=pltpu.HBM)
     return pl.pallas_call(
         project_kernel,
-        in_specs=[hbm, hbm, vmem],
+        in_specs=[hbm, hbm, hbm],
         out_specs=[vmem, vmem],
         out_shape=[table, table],
         scratch_shapes=[
             pltpu.VMEM((rows, width), jnp.float32),
             pltpu.VMEM((rows, hidden), jnp.float32),
+            pltpu.VMEM((width, hidden), jnp.bfloat16),
             pltpu.SemaphoreType.DMA((rows // PROJECT_STEP,)),
+            pltpu.SemaphoreType.DMA,
             pltpu.SemaphoreType.DMA,
         ],
         cost_estimate=pl.CostEstimate(

time: 62.1 us -> 62.1 us (level)
  Pallas kernels: 26.1 us -> 25.2 us
  waiting for transfers between devices: 19 us -> 19.8 us
  transfers between devices with their start and end apart: 2 -> 2, of which waited for: 2 -> 2; matrix products, arithmetic and copies ran while one was open for 0% -> 0% of each run, Pallas kernels for 24% -> 23%
where the time goes in v4:
time: 62.1 us; the launch traced here: 61.8 us
  Pallas kernels  25.2 us (41%)
  waiting for transfers between devices  19.8 us (32%)
  starting transfers between devices  16 us (26%)
  between operations  0.7 us (1%)
    all_to_all x1, waiting for transfers between devices, on_device(): lax.all_to_all(picked, 'nodes', split_axis=0, concat_axis=0, tiled=True)  13.1 us
    all_to_all x1, starting transfers between devices, on_device(): lax.all_to_all(wanted, 'nodes', split_axis=0, concat_axis=0, tiled=True)  11.5 us
    pallas_call x1, Pallas kernels, build_dense(): pl.pallas_call(dense_kernel, in_specs=[smem, smem, smem, hbm], out_specs=...  11.2 us
    pallas_call x1, Pallas kernels, combine(): pl.pallas_call(functools.partial(combine_kernel, req), in_specs=[vmem, hb...  6.88 us
    all_to_all x1, waiting for transfers between devices, on_device(): lax.all_to_all(wanted, 'nodes', split_axis=0, concat_axis=0, tiled=True)  6.79 us
    all_to_all x1, starting transfers between devices, on_device(): lax.all_to_all(picked, 'nodes', split_axis=0, concat_axis=0, tiled=True)  4.51 us
    pallas_call x1, Pallas kernels, pick_rows(): pl.pallas_call(functools.partial(pick_kernel, req, halo), in_specs=[vmem,...  2.96 us
    pallas_call x1, Pallas kernels, project(): pl.pallas_call(project_kernel, in_specs=[hbm, hbm, hbm], out_specs=[vmem,...  2.73 us
  transfers between devices with their start and end apart: 2, of which 2 were waited for; matrix products, arithmetic and copies ran while one was open for 0% of the time, Pallas kernels for 23%

profile of v4, /device:TPU:1, one launch (start us, length us, event | category | flops | bytes accessed | tf_op | source)
XLA Modules:
  0.0 61.8 jit_solution(5426051375663023552)
XLA Ops:
  0.0 1.4 %pack_ids.1 = s32[128,128]{1,0:T(8,128)} custom-call(s32[16,128]{1,0:T(8,128)} %bitcast.11, s32[8,128]{1,0:T(8,128)} %bitcast.12, s32[1,128]{1,0:T(1,128)} %req_count_ref.1, s32[1,128]{1,0:T(1,128)} %halo_count_ref.1), custom_call_target="tpu_custom_call" | custom-call | tf_op jit(solution)/shard_map/pack_ids/pallas_call | solution.py:33
  1.4 11.5 %all-to-all-start = ((s32[128,1,128]{2,1,0:T(1,128)}), s32[128,1,128]{2,1,0:T(1,128)S(1)}, u32[]{:S(2)}, u32[]{:S(2)}) async-start(s32[128,1,128]{2,1,0:T(1,128)} %bitcast.5), calls=%async_computation | async-start | bytes 131072 | tf_op jit(solution)/shard_map/all_to_all | solution.py:367
  13.0 2.7 %project.1 = (bf16[1024,256]{1,0:T(8,128)(2,1)S(1)}, bf16[1024,256]{1,0:T(8,128)(2,1)S(1)}) custom-call(f32[1024,768]{1,0:T(8,128)} %features_ref.1, f32[1024,256]{1,0:T(8,128)} %history_ref.1, bf16[768,256]{1,0:T(8,128)(2,1)} %w_in_ref.1), custom_call_target="tpu_custom_call" | custom-call | flops 402653184 | bytes 5242880 | tf_op jit(solution)/shard_map/project/pallas_call | solution.py:80
  15.7 6.8 %all-to-all-done = s32[128,1,128]{2,1,0:T(1,128)S(1)} async-done(((s32[128,1,128]{2,1,0:T(1,128)}), s32[128,1,128]{2,1,0:T(1,128)S(1)}, u32[]{:S(2)}, u32[]{:S(2)}) %all-to-all-start) | async-done | bytes 65568 | tf_op jit(solution)/shard_map/all_to_all | solution.py:367
  22.5 3.0 %pick_rows.1 = bf16[128,24,256]{2,1,0:T(8,128)(2,1)} custom-call(s32[128,128]{1,0:T(8,128)S(1)} %bitcast.10, bf16[1024,256]{1,0:T(8,128)(2,1)S(1)} %get-tuple-element.11.proj_ref, bf16[1024,256]{1,0:T(8,128)(2,1)S(1)} %get-tuple-element.12.hist_ref), custom_call_target="tpu_custom_call" | custom-call | flops 1610612736 | bytes 3145728 | tf_op jit(solution)/shard_map/pick_rows/pallas_call | solution.py:154
  25.4 4.5 %all-to-all-start.1 = ((bf16[128,24,256]{2,1,0:T(8,128)(2,1)}), bf16[128,24,256]{2,1,0:T(8,128)(2,1)S(1)}, u32[]{:S(2)}, u32[]{:S(2)}) async-start(bf16[128,24,256]{2,1,0:T(8,128)(2,1)} %pick_rows.1), calls=%async_computation.1 | async-start | bytes 3145728 | tf_op jit(solution)/shard_map/all_to_all | solution.py:371
  30.6 0.0 copy-start
  30.6 11.2 %build_dense.1 = (bf16[256,3072]{1,0:T(8,128)(2,1)S(1)}, bf16[1792,3072]{1,0:T(8,128)(2,1)}) custom-call(s32[512]{0:T(512)} %rows_ref.1, s32[512]{0:T(512)} %cols_ref.1, s32[1]{0:T(128)S(6)} %copy.14.used_ref, bf16[512,128,128]{2,1,0:T(8,128)(2,1)} %tiles_ref.1), custom_call_target="tpu_custom_call" | custom-call | flops 1048576 | bytes 31457280 | tf_op jit(solution)/shard_map/build_dense/pallas_call | solution.py:243
  41.8 13.1 %all-to-all-done.1.came_ref = bf16[128,24,256]{2,1,0:T(8,128)(2,1)S(1)} async-done(((bf16[128,24,256]{2,1,0:T(8,128)(2,1)}), bf16[128,24,256]{2,1,0:T(8,128)(2,1)S(1)}, u32[]{:S(2)}, u32[]{:S(2)}) %all-to-all-start.1) | async-done | bytes 1572896 | tf_op jit(solution)/shard_map/all_to_all | solution.py:371
  54.9 0.0 copy-done
  54.9 6.9 %combine.1 = bf16[2048,256]{1,0:T(8,128)(2,1)} custom-call(bf16[256,3072]{1,0:T(8,128)(2,1)S(1)} %get-tuple-element.14.kept_ref, bf16[1792,3072]{1,0:T(8,128)(2,1)} %get-tuple-element.15.dense_ref, bf16[128,24,256]{2,1,0:T(8,128)(2,1)S(1)} %all-to-all-done.1.came_ref, bf16[256,256]{1,0:T(8,128)(2,1)S(1)} %copy-done), custom_call_target="tpu_custom_call" | custom-call | flops 3221225472 | bytes 16777216 | tf_op jit(solution)/shard_map/combine/pallas_call | solution.py:328
Async XLA Ops:
  1.4 21.0 %all-to-all-start = ((s32[128,1,128]{2,1,0:T(1,128)}), s32[128,1,128]{2,1,0:T(1,128)S(1)}, u32[]{:S(2)}, u32[]{:S(2)}) async-start(s32[128,1,128]{2,1,0:T(1,128)} %bitcast.5), calls=%async_computation | async-start | bytes 131072 | tf_op jit(solution)/shard_map/all_to_all | solution.py:367
  25.4 29.4 %all-to-all-start.1 = ((bf16[128,24,256]{2,1,0:T(8,128)(2,1)}), bf16[128,24,256]{2,1,0:T(8,128)(2,1)S(1)}, u32[]{:S(2)}, u32[]{:S(2)}) async-start(bf16[128,24,256]{2,1,0:T(8,128)(2,1)} %pick_rows.1), calls=%async_computation.1 | async-start | bytes 3145728 | tf_op jit(solution)/shard_map/all_to_all | solution.py:371
  30.6 24.3 %copy-start = (bf16[256,256]{1,0:T(8,128)(2,1)S(1)}, bf16[256,256]{1,0:T(8,128)(2,1)}, u32[]{:S(2)}) copy-start(bf16[256,256]{1,0:T(8,128)(2,1)} %w_ref.1) | copy-start | bytes 393220

commit v5 on v4

--- a/solution.py
+++ b/solution.py
@@ -11,7 +11,7 @@
 TILE_CHUNKS = 8
 TILE_UNROLL = 4
 OUT_SLOTS = 8
-PICK_PARTS = 2
+PICK_CUTS = (0, 2, 4, 6, 7, 8)
 ROWS_STEP = 512
 KEPT_ROWS = 256
 PROJECT_STEP = 512
@@ -98,7 +98,7 @@
     )(features, history, w_in)
 
 
-def pick_kernel(req, halo, ids_ref, proj_ref, hist_ref, out_ref, req_ref, halo_ref, sem):
+def pick_kernel(req, halo, ids_ref, proj_ref, hist_ref, out_ref, held_ref, sem):
     count = ids_ref.shape[0]
     rows = proj_ref.shape[0]
     turned = ids_ref[...].T
@@ -125,23 +125,18 @@
         )
         return picked.astype(jnp.bfloat16).reshape(last - first, size, -1)
 
+    def send(first, last, k):
+        at = pl.ds(first, last - first)
+        return pltpu.make_async_copy(held_ref.at[at], out_ref.at[at], sem.at[k])
+
+    cuts = [count * part // 8 for part in PICK_CUTS]
     copies = []
-
-    def send(held_ref, start, size, first, last):
-        copy = pltpu.make_async_copy(
-            held_ref.at[first:last],
-            out_ref.at[first:last, start : start + size, :],
-            sem.at[len(copies)],
-        )
+    for k, (first, last) in enumerate(zip(cuts[:-1], cuts[1:])):
+        held_ref[first:last, :req, :] = pick(proj_ref, 0, req, first, last)
+        held_ref[first:last, req:, :] = pick(hist_ref, req, halo, first, last)
+        copy = send(first, last, k)
         copy.start()
         copies.append(copy)
-
-    halo_ref[...] = pick(hist_ref, req, halo, 0, count)
-    send(halo_ref, req, halo, 0, count)
-    part = count // PICK_PARTS
-    for first in range(0, count, part):
-        req_ref[first : first + part] = pick(proj_ref, 0, req, first, first + part)
-        send(req_ref, 0, req, first, first + part)
     for copy in copies:
         copy.wait()
 
@@ -157,9 +152,8 @@
         out_specs=pl.BlockSpec(memory_space=pltpu.HBM),
         out_shape=jax.ShapeDtypeStruct((count, req + halo, hidden), jnp.bfloat16),
         scratch_shapes=[
-            pltpu.VMEM((count, req, hidden), jnp.bfloat16),
-            pltpu.VMEM((count, halo, hidden), jnp.bfloat16),
-            pltpu.SemaphoreType.DMA((1 + PICK_PARTS,)),
+            pltpu.VMEM((count, req + halo, hidden), jnp.bfloat16),
+            pltpu.SemaphoreType.DMA((len(PICK_CUTS) - 1,)),
         ],
         cost_estimate=pl.CostEstimate(flops=flops, bytes_accessed=3 << 20, transcendentals=0),
         compiler_params=pltpu.CompilerParams(vmem_limit_bytes=24 << 20),

time: 62.1 us -> 61.8 us (level)
  no operation moved by 1% of the time
where the time goes in v5:
time: 61.8 us; the launch traced here: 61.5 us
  Pallas kernels  25 us (40%)
  waiting for transfers between devices  19.8 us (32%)
  starting transfers between devices  16 us (26%)
  between operations  0.7 us (1%)
    all_to_all x1, waiting for transfers between devices, on_device(): lax.all_to_all(picked, 'nodes', split_axis=0, concat_axis=0, tiled=True)  13.1 us
    all_to_all x1, starting transfers between devices, on_device(): lax.all_to_all(wanted, 'nodes', split_axis=0, concat_axis=0, tiled=True)  11.5 us
    pallas_call x1, Pallas kernels, build_dense(): pl.pallas_call(dense_kernel, in_specs=[smem, smem, smem, hbm], out_specs=...  11.2 us
    pallas_call x1, Pallas kernels, combine(): pl.pallas_call(functools.partial(combine_kernel, req), in_specs=[vmem, hb...  6.88 us
    all_to_all x1, waiting for transfers between devices, on_device(): lax.all_to_all(wanted, 'nodes', split_axis=0, concat_axis=0, tiled=True)  6.79 us
    all_to_all x1, starting transfers between devices, on_device(): lax.all_to_all(picked, 'nodes', split_axis=0, concat_axis=0, tiled=True)  4.5 us
    pallas_call x1, Pallas kernels, project(): pl.pallas_call(project_kernel, in_specs=[hbm, hbm, hbm], out_specs=[vmem,...  2.73 us
    pallas_call x1, Pallas kernels, pick_rows(): pl.pallas_call(functools.partial(pick_kernel, req, halo), in_specs=[vmem,...  2.73 us
  transfers between devices with their start and end apart: 2, of which 2 were waited for; matrix products, arithmetic and copies ran while one was open for 0% of the time, Pallas kernels for 23%

profile of v5, /device:TPU:1, one launch (start us, length us, event | category | flops | bytes accessed | tf_op | source)
XLA Modules:
  0.0 61.5 jit_solution(6293832760267108710)
XLA Ops:
  0.0 1.4 %pack_ids.1 = s32[128,128]{1,0:T(8,128)} custom-call(s32[16,128]{1,0:T(8,128)} %bitcast.11, s32[8,128]{1,0:T(8,128)} %bitcast.12, s32[1,128]{1,0:T(1,128)} %req_count_ref.1, s32[1,128]{1,0:T(1,128)} %halo_count_ref.1), custom_call_target="tpu_custom_call" | custom-call | tf_op jit(solution)/shard_map/pack_ids/pallas_call | solution.py:33
  1.4 11.5 %all-to-all-start = ((s32[128,1,128]{2,1,0:T(1,128)}), s32[128,1,128]{2,1,0:T(1,128)S(1)}, u32[]{:S(2)}, u32[]{:S(2)}) async-start(s32[128,1,128]{2,1,0:T(1,128)} %bitcast.5), calls=%async_computation | async-start | bytes 131072 | tf_op jit(solution)/shard_map/all_to_all | solution.py:361
  13.0 2.7 %project.1 = (bf16[1024,256]{1,0:T(8,128)(2,1)S(1)}, bf16[1024,256]{1,0:T(8,128)(2,1)S(1)}) custom-call(f32[1024,768]{1,0:T(8,128)} %features_ref.1, f32[1024,256]{1,0:T(8,128)} %history_ref.1, bf16[768,256]{1,0:T(8,128)(2,1)} %w_in_ref.1), custom_call_target="tpu_custom_call" | custom-call | flops 402653184 | bytes 5242880 | tf_op jit(solution)/shard_map/project/pallas_call | solution.py:80
  15.7 6.8 %all-to-all-done = s32[128,1,128]{2,1,0:T(1,128)S(1)} async-done(((s32[128,1,128]{2,1,0:T(1,128)}), s32[128,1,128]{2,1,0:T(1,128)S(1)}, u32[]{:S(2)}, u32[]{:S(2)}) %all-to-all-start) | async-done | bytes 65568 | tf_op jit(solution)/shard_map/all_to_all | solution.py:361
  22.5 2.7 %pick_rows.1 = bf16[128,24,256]{2,1,0:T(8,128)(2,1)} custom-call(s32[128,128]{1,0:T(8,128)S(1)} %bitcast.10, bf16[1024,256]{1,0:T(8,128)(2,1)S(1)} %get-tuple-element.11.proj_ref, bf16[1024,256]{1,0:T(8,128)(2,1)S(1)} %get-tuple-element.12.hist_ref), custom_call_target="tpu_custom_call" | custom-call | flops 1610612736 | bytes 3145728 | tf_op jit(solution)/shard_map/pick_rows/pallas_call | solution.py:149
  25.2 4.5 %all-to-all-start.1 = ((bf16[128,24,256]{2,1,0:T(8,128)(2,1)}), bf16[128,24,256]{2,1,0:T(8,128)(2,1)S(1)}, u32[]{:S(2)}, u32[]{:S(2)}) async-start(bf16[128,24,256]{2,1,0:T(8,128)(2,1)} %pick_rows.1), calls=%async_computation.1 | async-start | bytes 3145728 | tf_op jit(solution)/shard_map/all_to_all | solution.py:365
  30.4 0.0 copy-start
  30.4 11.2 %build_dense.1 = (bf16[256,3072]{1,0:T(8,128)(2,1)S(1)}, bf16[1792,3072]{1,0:T(8,128)(2,1)}) custom-call(s32[512]{0:T(512)} %rows_ref.1, s32[512]{0:T(512)} %cols_ref.1, s32[1]{0:T(128)S(6)} %copy.14.used_ref, bf16[512,128,128]{2,1,0:T(8,128)(2,1)} %tiles_ref.1), custom_call_target="tpu_custom_call" | custom-call | flops 1048576 | bytes 31457280 | tf_op jit(solution)/shard_map/build_dense/pallas_call | solution.py:237
  41.6 13.1 %all-to-all-done.1.came_ref = bf16[128,24,256]{2,1,0:T(8,128)(2,1)S(1)} async-done(((bf16[128,24,256]{2,1,0:T(8,128)(2,1)}), bf16[128,24,256]{2,1,0:T(8,128)(2,1)S(1)}, u32[]{:S(2)}, u32[]{:S(2)}) %all-to-all-start.1) | async-done | bytes 1572896 | tf_op jit(solution)/shard_map/all_to_all | solution.py:365
  54.7 0.0 copy-done
  54.7 6.9 %combine.1 = bf16[2048,256]{1,0:T(8,128)(2,1)} custom-call(bf16[256,3072]{1,0:T(8,128)(2,1)S(1)} %get-tuple-element.14.kept_ref, bf16[1792,3072]{1,0:T(8,128)(2,1)} %get-tuple-element.15.dense_ref, bf16[128,24,256]{2,1,0:T(8,128)(2,1)S(1)} %all-to-all-done.1.came_ref, bf16[256,256]{1,0:T(8,128)(2,1)S(1)} %copy-done), custom_call_target="tpu_custom_call" | custom-call | flops 3221225472 | bytes 16777216 | tf_op jit(solution)/shard_map/combine/pallas_call | solution.py:322
Async XLA Ops:
  1.4 21.0 %all-to-all-start = ((s32[128,1,128]{2,1,0:T(1,128)}), s32[128,1,128]{2,1,0:T(1,128)S(1)}, u32[]{:S(2)}, u32[]{:S(2)}) async-start(s32[128,1,128]{2,1,0:T(1,128)} %bitcast.5), calls=%async_computation | async-start | bytes 131072 | tf_op jit(solution)/shard_map/all_to_all | solution.py:361
  25.2 29.4 %all-to-all-start.1 = ((bf16[128,24,256]{2,1,0:T(8,128)(2,1)}), bf16[128,24,256]{2,1,0:T(8,128)(2,1)S(1)}, u32[]{:S(2)}, u32[]{:S(2)}) async-start(bf16[128,24,256]{2,1,0:T(8,128)(2,1)} %pick_rows.1), calls=%async_computation.1 | async-start | bytes 3145728 | tf_op jit(solution)/shard_map/all_to_all | solution.py:365
  30.4 24.3 %copy-start = (bf16[256,256]{1,0:T(8,128)(2,1)S(1)}, bf16[256,256]{1,0:T(8,128)(2,1)}, u32[]{:S(2)}) copy-start(bf16[256,256]{1,0:T(8,128)(2,1)} %w_ref.1) | copy-start | bytes 393220

commit v6 on v5

--- a/solution.py
+++ b/solution.py
@@ -257,7 +257,7 @@
 
 def combine_kernel(
     req, kept_ref, dense_ref, came_ref, w_ref, out_ref,
-    held_ref, source_ref, stage_ref, kept_sem, in_sem, out_sem,
+    held_ref, source_ref, mixed_ref, stage_ref, kept_sem, in_sem, out_sem,
 ):
     owners, slots, hidden = came_ref.shape
     nodes = owners * req
@@ -286,6 +286,13 @@
     fetch_step(1).start()
     source_ref[:nodes] = came_ref[:, :req, :].reshape(nodes, hidden)
     source_ref[nodes:] = came_ref[:, req:, :].reshape(owners * (slots - req), hidden)
+
+    @pl.loop(0, 3)
+    def _(j):
+        at = pl.ds(pl.multiple_of(j * 1024, 1024), 1024)
+        mixed_ref[at] = jnp.dot(
+            source_ref[at], w_ref[...], preferred_element_type=jnp.float32
+        ).astype(jnp.bfloat16)
 
     @pl.loop(0, steps)
     def _(k):
@@ -303,8 +310,7 @@
             fetch_step(k + 2).start()
 
         at = pl.ds(pl.multiple_of(k * step, step), step)
-        total = jnp.dot(held_ref[at], source_ref[...], preferred_element_type=jnp.float32)
-        mixed = jnp.dot(total.astype(jnp.bfloat16), w_ref[...], preferred_element_type=jnp.float32)
+        mixed = jnp.dot(held_ref[at], mixed_ref[...], preferred_element_type=jnp.float32)
         own = source_ref[at].astype(jnp.float32)
         stage_ref[at] = jnp.maximum(mixed + own, 0.0).astype(jnp.bfloat16)
         flush(k).start()
@@ -326,6 +332,7 @@
         out_shape=jax.ShapeDtypeStruct((nodes, hidden), jnp.bfloat16),
         scratch_shapes=[
             pltpu.VMEM((nodes, width), jnp.bfloat16),
+            pltpu.VMEM((width, hidden), jnp.bfloat16),
             pltpu.VMEM((width, hidden), jnp.bfloat16),
             pltpu.VMEM((nodes, hidden), jnp.bfloat16),
             pltpu.SemaphoreType.DMA,

time: 61.8 us -> 61.3 us (level)
  no operation moved by 1% of the time
where the time goes in v6:
time: 61.3 us; the launch traced here: 61 us
  Pallas kernels  24.5 us (40%)
  waiting for transfers between devices  19.8 us (32%)
  starting transfers between devices  16 us (26%)
  between operations  0.7 us (1%)
    all_to_all x1, waiting for transfers between devices, on_device(): lax.all_to_all(picked, 'nodes', split_axis=0, concat_axis=0, tiled=True)  13.1 us
    all_to_all x1, starting transfers between devices, on_device(): lax.all_to_all(wanted, 'nodes', split_axis=0, concat_axis=0, tiled=True)  11.5 us
    pallas_call x1, Pallas kernels, build_dense(): pl.pallas_call(dense_kernel, in_specs=[smem, smem, smem, hbm], out_specs=...  11.2 us
    all_to_all x1, waiting for transfers between devices, on_device(): lax.all_to_all(wanted, 'nodes', split_axis=0, concat_axis=0, tiled=True)  6.79 us
    pallas_call x1, Pallas kernels, combine(): pl.pallas_call(functools.partial(combine_kernel, req), in_specs=[vmem, hb...  6.34 us
    all_to_all x1, starting transfers between devices, on_device(): lax.all_to_all(picked, 'nodes', split_axis=0, concat_axis=0, tiled=True)  4.5 us
    pallas_call x1, Pallas kernels, project(): pl.pallas_call(project_kernel, in_specs=[hbm, hbm, hbm], out_specs=[vmem,...  2.73 us
    pallas_call x1, Pallas kernels, pick_rows(): pl.pallas_call(functools.partial(pick_kernel, req, halo), in_specs=[vmem,...  2.73 us
  transfers between devices with their start and end apart: 2, of which 2 were waited for; matrix products, arithmetic and copies ran while one was open for 0% of the time, Pallas kernels for 23%

profile of v6, /device:TPU:1, one launch (start us, length us, event | category | flops | bytes accessed | tf_op | source)
XLA Modules:
  0.0 61.0 jit_solution(9082315515979563916)
XLA Ops:
  0.0 1.4 %pack_ids.1 = s32[128,128]{1,0:T(8,128)} custom-call(s32[16,128]{1,0:T(8,128)} %bitcast.11, s32[8,128]{1,0:T(8,128)} %bitcast.12, s32[1,128]{1,0:T(1,128)} %req_count_ref.1, s32[1,128]{1,0:T(1,128)} %halo_count_ref.1), custom_call_target="tpu_custom_call" | custom-call | tf_op jit(solution)/shard_map/pack_ids/pallas_call | solution.py:33
  1.4 11.5 %all-to-all-start = ((s32[128,1,128]{2,1,0:T(1,128)}), s32[128,1,128]{2,1,0:T(1,128)S(1)}, u32[]{:S(2)}, u32[]{:S(2)}) async-start(s32[128,1,128]{2,1,0:T(1,128)} %bitcast.5), calls=%async_computation | async-start | bytes 131072 | tf_op jit(solution)/shard_map/all_to_all | solution.py:368
  13.0 2.7 %project.1 = (bf16[1024,256]{1,0:T(8,128)(2,1)S(1)}, bf16[1024,256]{1,0:T(8,128)(2,1)S(1)}) custom-call(f32[1024,768]{1,0:T(8,128)} %features_ref.1, f32[1024,256]{1,0:T(8,128)} %history_ref.1, bf16[768,256]{1,0:T(8,128)(2,1)} %w_in_ref.1), custom_call_target="tpu_custom_call" | custom-call | flops 402653184 | bytes 5242880 | tf_op jit(solution)/shard_map/project/pallas_call | solution.py:80
  15.7 6.8 %all-to-all-done = s32[128,1,128]{2,1,0:T(1,128)S(1)} async-done(((s32[128,1,128]{2,1,0:T(1,128)}), s32[128,1,128]{2,1,0:T(1,128)S(1)}, u32[]{:S(2)}, u32[]{:S(2)}) %all-to-all-start) | async-done | bytes 65568 | tf_op jit(solution)/shard_map/all_to_all | solution.py:368
  22.5 2.7 %pick_rows.1 = bf16[128,24,256]{2,1,0:T(8,128)(2,1)} custom-call(s32[128,128]{1,0:T(8,128)S(1)} %bitcast.10, bf16[1024,256]{1,0:T(8,128)(2,1)S(1)} %get-tuple-element.11.proj_ref, bf16[1024,256]{1,0:T(8,128)(2,1)S(1)} %get-tuple-element.12.hist_ref), custom_call_target="tpu_custom_call" | custom-call | flops 1610612736 | bytes 3145728 | tf_op jit(solution)/shard_map/pick_rows/pallas_call | solution.py:149
  25.2 4.5 %all-to-all-start.1 = ((bf16[128,24,256]{2,1,0:T(8,128)(2,1)}), bf16[128,24,256]{2,1,0:T(8,128)(2,1)S(1)}, u32[]{:S(2)}, u32[]{:S(2)}) async-start(bf16[128,24,256]{2,1,0:T(8,128)(2,1)} %pick_rows.1), calls=%async_computation.1 | async-start | bytes 3145728 | tf_op jit(solution)/shard_map/all_to_all | solution.py:372
  30.4 0.0 copy-start
  30.4 11.2 %build_dense.1 = (bf16[256,3072]{1,0:T(8,128)(2,1)S(1)}, bf16[1792,3072]{1,0:T(8,128)(2,1)}) custom-call(s32[512]{0:T(512)} %rows_ref.1, s32[512]{0:T(512)} %cols_ref.1, s32[1]{0:T(128)S(6)} %copy.14.used_ref, bf16[512,128,128]{2,1,0:T(8,128)(2,1)} %tiles_ref.1), custom_call_target="tpu_custom_call" | custom-call | flops 1048576 | bytes 31457280 | tf_op jit(solution)/shard_map/build_dense/pallas_call | solution.py:237
  41.6 13.1 %all-to-all-done.1.came_ref = bf16[128,24,256]{2,1,0:T(8,128)(2,1)S(1)} async-done(((bf16[128,24,256]{2,1,0:T(8,128)(2,1)}), bf16[128,24,256]{2,1,0:T(8,128)(2,1)S(1)}, u32[]{:S(2)}, u32[]{:S(2)}) %all-to-all-start.1) | async-done | bytes 1572896 | tf_op jit(solution)/shard_map/all_to_all | solution.py:372
  54.7 0.0 copy-done
  54.7 6.3 %combine.1 = bf16[2048,256]{1,0:T(8,128)(2,1)} custom-call(bf16[256,3072]{1,0:T(8,128)(2,1)S(1)} %get-tuple-element.14.kept_ref, bf16[1792,3072]{1,0:T(8,128)(2,1)} %get-tuple-element.15.dense_ref, bf16[128,24,256]{2,1,0:T(8,128)(2,1)S(1)} %all-to-all-done.1.came_ref, bf16[256,256]{1,0:T(8,128)(2,1)S(1)} %copy-done), custom_call_target="tpu_custom_call" | custom-call | flops 3221225472 | bytes 16777216 | tf_op jit(solution)/shard_map/combine/pallas_call | solution.py:328
Async XLA Ops:
  1.4 21.0 %all-to-all-start = ((s32[128,1,128]{2,1,0:T(1,128)}), s32[128,1,128]{2,1,0:T(1,128)S(1)}, u32[]{:S(2)}, u32[]{:S(2)}) async-start(s32[128,1,128]{2,1,0:T(1,128)} %bitcast.5), calls=%async_computation | async-start | bytes 131072 | tf_op jit(solution)/shard_map/all_to_all | solution.py:368
  25.2 29.4 %all-to-all-start.1 = ((bf16[128,24,256]{2,1,0:T(8,128)(2,1)}), bf16[128,24,256]{2,1,0:T(8,128)(2,1)S(1)}, u32[]{:S(2)}, u32[]{:S(2)}) async-start(bf16[128,24,256]{2,1,0:T(8,128)(2,1)} %pick_rows.1), calls=%async_computation.1 | async-start | bytes 3145728 | tf_op jit(solution)/shard_map/all_to_all | solution.py:372
  30.4 24.3 %copy-start = (bf16[256,256]{1,0:T(8,128)(2,1)S(1)}, bf16[256,256]{1,0:T(8,128)(2,1)}, u32[]{:S(2)}) copy-start(bf16[256,256]{1,0:T(8,128)(2,1)} %w_ref.1) | copy-start | bytes 393220

commit v7 on v6

--- a/solution.py
+++ b/solution.py
@@ -257,7 +257,7 @@
 
 def combine_kernel(
     req, kept_ref, dense_ref, came_ref, w_ref, out_ref,
-    held_ref, source_ref, mixed_ref, stage_ref, kept_sem, in_sem, out_sem,
+    held_ref, source_ref, mixed_ref, stage_ref, in_sem, out_sem,
 ):
     owners, slots, hidden = came_ref.shape
     nodes = owners * req
@@ -274,7 +274,6 @@
     def fetch_step(k):
         return fetch(k * step, step, k)
 
-    near = pltpu.make_async_copy(kept_ref, held_ref.at[pl.ds(0, kept)], kept_sem)
     start = fetch(kept, step - kept, 0)
 
     def flush(k):
@@ -282,8 +281,9 @@
         return pltpu.make_async_copy(stage_ref.at[at], out_ref.at[at], out_sem.at[k])
 
     start.start()
-    near.start()
-    fetch_step(1).start()
+    held_ref[:kept] = kept_ref[...]
+    for k in range(1, steps):
+        fetch_step(k).start()
     source_ref[:nodes] = came_ref[:, :req, :].reshape(nodes, hidden)
     source_ref[nodes:] = came_ref[:, req:, :].reshape(owners * (slots - req), hidden)
 
@@ -299,15 +299,10 @@
         @pl.when(k == 0)
         def _():
             start.wait()
-            near.wait()
 
         @pl.when(k > 0)
         def _():
             fetch_step(k).wait()
-
-        @pl.when(k + 2 < steps)
-        def _():
-            fetch_step(k + 2).start()
 
         at = pl.ds(pl.multiple_of(k * step, step), step)
         mixed = jnp.dot(held_ref[at], mixed_ref[...], preferred_element_type=jnp.float32)
@@ -335,7 +330,6 @@
             pltpu.VMEM((width, hidden), jnp.bfloat16),
             pltpu.VMEM((width, hidden), jnp.bfloat16),
             pltpu.VMEM((nodes, hidden), jnp.bfloat16),
-            pltpu.SemaphoreType.DMA,
             pltpu.SemaphoreType.DMA((nodes // ROWS_STEP,)),
             pltpu.SemaphoreType.DMA((nodes // ROWS_STEP,)),
         ],

time: 61.3 us -> 61 us (level)
  transfers between devices with their start and end apart: 2 -> 2, of which waited for: 2 -> 2; matrix products, arithmetic and copies ran while one was open for 0% -> 0% of each run, Pallas kernels for 23% -> 24%
where the time goes in v7:
time: 61 us; the launch traced here: 60.8 us
  Pallas kernels  24.7 us (40%)
  waiting for transfers between devices  19.4 us (32%)
  starting transfers between devices  16 us (26%)
  between operations  0.7 us (1%)
    all_to_all x1, waiting for transfers between devices, on_device(): lax.all_to_all(picked, 'nodes', split_axis=0, concat_axis=0, tiled=True)  12.6 us
    pallas_call x1, Pallas kernels, build_dense(): pl.pallas_call(dense_kernel, in_specs=[smem, smem, smem, hbm], out_specs=...  11.7 us
    all_to_all x1, starting transfers between devices, on_device(): lax.all_to_all(wanted, 'nodes', split_axis=0, concat_axis=0, tiled=True)  11.5 us
    all_to_all x1, waiting for transfers between devices, on_device(): lax.all_to_all(wanted, 'nodes', split_axis=0, concat_axis=0, tiled=True)  6.79 us
    pallas_call x1, Pallas kernels, combine(): pl.pallas_call(functools.partial(combine_kernel, req), in_specs=[vmem, hb...  6.1 us
    all_to_all x1, starting transfers between devices, on_device(): lax.all_to_all(picked, 'nodes', split_axis=0, concat_axis=0, tiled=True)  4.5 us
    pallas_call x1, Pallas kernels, project(): pl.pallas_call(project_kernel, in_specs=[hbm, hbm, hbm], out_specs=[vmem,...  2.73 us
    pallas_call x1, Pallas kernels, pick_rows(): pl.pallas_call(functools.partial(pick_kernel, req, halo), in_specs=[vmem,...  2.73 us
  transfers between devices with their start and end apart: 2, of which 2 were waited for; matrix products, arithmetic and copies ran while one was open for 0% of the time, Pallas kernels for 24%

profile of v7, /device:TPU:1, one launch (start us, length us, event | category | flops | bytes accessed | tf_op | source)
XLA Modules:
  0.0 60.8 jit_solution(4101349743985012061)
XLA Ops:
  0.0 1.4 %pack_ids.1 = s32[128,128]{1,0:T(8,128)} custom-call(s32[16,128]{1,0:T(8,128)} %bitcast.11, s32[8,128]{1,0:T(8,128)} %bitcast.12, s32[1,128]{1,0:T(1,128)} %req_count_ref.1, s32[1,128]{1,0:T(1,128)} %halo_count_ref.1), custom_call_target="tpu_custom_call" | custom-call | tf_op jit(solution)/shard_map/pack_ids/pallas_call | solution.py:33
  1.4 11.5 %all-to-all-start = ((s32[128,1,128]{2,1,0:T(1,128)}), s32[128,1,128]{2,1,0:T(1,128)S(1)}, u32[]{:S(2)}, u32[]{:S(2)}) async-start(s32[128,1,128]{2,1,0:T(1,128)} %bitcast.5), calls=%async_computation | async-start | bytes 131072 | tf_op jit(solution)/shard_map/all_to_all | solution.py:362
  13.0 2.7 %project.1 = (bf16[1024,256]{1,0:T(8,128)(2,1)S(1)}, bf16[1024,256]{1,0:T(8,128)(2,1)S(1)}) custom-call(f32[1024,768]{1,0:T(8,128)} %features_ref.1, f32[1024,256]{1,0:T(8,128)} %history_ref.1, bf16[768,256]{1,0:T(8,128)(2,1)} %w_in_ref.1), custom_call_target="tpu_custom_call" | custom-call | flops 402653184 | bytes 5242880 | tf_op jit(solution)/shard_map/project/pallas_call | solution.py:80
  15.7 6.8 %all-to-all-done = s32[128,1,128]{2,1,0:T(1,128)S(1)} async-done(((s32[128,1,128]{2,1,0:T(1,128)}), s32[128,1,128]{2,1,0:T(1,128)S(1)}, u32[]{:S(2)}, u32[]{:S(2)}) %all-to-all-start) | async-done | bytes 65568 | tf_op jit(solution)/shard_map/all_to_all | solution.py:362
  22.5 2.7 %pick_rows.1 = bf16[128,24,256]{2,1,0:T(8,128)(2,1)} custom-call(s32[128,128]{1,0:T(8,128)S(1)} %bitcast.10, bf16[1024,256]{1,0:T(8,128)(2,1)S(1)} %get-tuple-element.11.proj_ref, bf16[1024,256]{1,0:T(8,128)(2,1)S(1)} %get-tuple-element.12.hist_ref), custom_call_target="tpu_custom_call" | custom-call | flops 1610612736 | bytes 3145728 | tf_op jit(solution)/shard_map/pick_rows/pallas_call | solution.py:149
  25.2 4.5 %all-to-all-start.1 = ((bf16[128,24,256]{2,1,0:T(8,128)(2,1)}), bf16[128,24,256]{2,1,0:T(8,128)(2,1)S(1)}, u32[]{:S(2)}, u32[]{:S(2)}) async-start(bf16[128,24,256]{2,1,0:T(8,128)(2,1)} %pick_rows.1), calls=%async_computation.1 | async-start | bytes 3145728 | tf_op jit(solution)/shard_map/all_to_all | solution.py:366
  30.4 0.0 copy-start
  30.4 11.7 %build_dense.1 = (bf16[256,3072]{1,0:T(8,128)(2,1)S(1)}, bf16[1792,3072]{1,0:T(8,128)(2,1)}) custom-call(s32[512]{0:T(512)} %rows_ref.1, s32[512]{0:T(512)} %cols_ref.1, s32[1]{0:T(128)S(6)} %copy.14.used_ref, bf16[512,128,128]{2,1,0:T(8,128)(2,1)} %tiles_ref.1), custom_call_target="tpu_custom_call" | custom-call | flops 1048576 | bytes 31457280 | tf_op jit(solution)/shard_map/build_dense/pallas_call | solution.py:237
  42.1 12.6 %all-to-all-done.1.came_ref = bf16[128,24,256]{2,1,0:T(8,128)(2,1)S(1)} async-done(((bf16[128,24,256]{2,1,0:T(8,128)(2,1)}), bf16[128,24,256]{2,1,0:T(8,128)(2,1)S(1)}, u32[]{:S(2)}, u32[]{:S(2)}) %all-to-all-start.1) | async-done | bytes 1572896 | tf_op jit(solution)/shard_map/all_to_all | solution.py:366
  54.7 0.0 copy-done
  54.7 6.1 %combine.1 = bf16[2048,256]{1,0:T(8,128)(2,1)} custom-call(bf16[256,3072]{1,0:T(8,128)(2,1)S(1)} %get-tuple-element.14.kept_ref, bf16[1792,3072]{1,0:T(8,128)(2,1)} %get-tuple-element.15.dense_ref, bf16[128,24,256]{2,1,0:T(8,128)(2,1)S(1)} %all-to-all-done.1.came_ref, bf16[256,256]{1,0:T(8,128)(2,1)S(1)} %copy-done), custom_call_target="tpu_custom_call" | custom-call | flops 3221225472 | bytes 16777216 | tf_op jit(solution)/shard_map/combine/pallas_call | solution.py:323
Async XLA Ops:
  1.4 21.0 %all-to-all-start = ((s32[128,1,128]{2,1,0:T(1,128)}), s32[128,1,128]{2,1,0:T(1,128)S(1)}, u32[]{:S(2)}, u32[]{:S(2)}) async-start(s32[128,1,128]{2,1,0:T(1,128)} %bitcast.5), calls=%async_computation | async-start | bytes 131072 | tf_op jit(solution)/shard_map/all_to_all | solution.py:362
  25.2 29.4 %all-to-all-start.1 = ((bf16[128,24,256]{2,1,0:T(8,128)(2,1)}), bf16[128,24,256]{2,1,0:T(8,128)(2,1)S(1)}, u32[]{:S(2)}, u32[]{:S(2)}) async-start(bf16[128,24,256]{2,1,0:T(8,128)(2,1)} %pick_rows.1), calls=%async_computation.1 | async-start | bytes 3145728 | tf_op jit(solution)/shard_map/all_to_all | solution.py:366
  30.4 24.3 %copy-start = (bf16[256,256]{1,0:T(8,128)(2,1)S(1)}, bf16[256,256]{1,0:T(8,128)(2,1)}, u32[]{:S(2)}) copy-start(bf16[256,256]{1,0:T(8,128)(2,1)} %w_ref.1) | copy-start | bytes 393220

commit v8 on v7

--- a/solution.py
+++ b/solution.py
@@ -281,9 +281,9 @@
         return pltpu.make_async_copy(stage_ref.at[at], out_ref.at[at], out_sem.at[k])
 
     start.start()
-    held_ref[:kept] = kept_ref[...]
     for k in range(1, steps):
         fetch_step(k).start()
+    held_ref[:kept] = kept_ref[...]
     source_ref[:nodes] = came_ref[:, :req, :].reshape(nodes, hidden)
     source_ref[nodes:] = came_ref[:, req:, :].reshape(owners * (slots - req), hidden)
 

time: 61 us -> 61 us (level)
  transfers between devices with their start and end apart: 2 -> 2, of which waited for: 2 -> 2; matrix products, arithmetic and copies ran while one was open for 0% -> 0% of each run, Pallas kernels for 24% -> 23%
where the time goes in v8:
time: 61 us; the launch traced here: 60.8 us
  Pallas kernels  24.2 us (40%)
  waiting for transfers between devices  19.8 us (32%)
  starting transfers between devices  16 us (26%)
  between operations  0.7 us (1%)
    all_to_all x1, waiting for transfers between devices, on_device(): lax.all_to_all(picked, 'nodes', split_axis=0, concat_axis=0, tiled=True)  13.1 us
    all_to_all x1, starting transfers between devices, on_device(): lax.all_to_all(wanted, 'nodes', split_axis=0, concat_axis=0, tiled=True)  11.5 us
    pallas_call x1, Pallas kernels, build_dense(): pl.pallas_call(dense_kernel, in_specs=[smem, smem, smem, hbm], out_specs=...  11.2 us
    all_to_all x1, waiting for transfers between devices, on_device(): lax.all_to_all(wanted, 'nodes', split_axis=0, concat_axis=0, tiled=True)  6.79 us
    pallas_call x1, Pallas kernels, combine(): pl.pallas_call(functools.partial(combine_kernel, req), in_specs=[vmem, hb...  6.1 us
    all_to_all x1, starting transfers between devices, on_device(): lax.all_to_all(picked, 'nodes', split_axis=0, concat_axis=0, tiled=True)  4.5 us
    pallas_call x1, Pallas kernels, project(): pl.pallas_call(project_kernel, in_specs=[hbm, hbm, hbm], out_specs=[vmem,...  2.73 us
    pallas_call x1, Pallas kernels, pick_rows(): pl.pallas_call(functools.partial(pick_kernel, req, halo), in_specs=[vmem,...  2.73 us
  transfers between devices with their start and end apart: 2, of which 2 were waited for; matrix products, arithmetic and copies ran while one was open for 0% of the time, Pallas kernels for 23%

profile of v8, /device:TPU:1, one launch (start us, length us, event | category | flops | bytes accessed | tf_op | source)
XLA Modules:
  0.0 60.8 jit_solution(1556987418248893040)
XLA Ops:
  0.0 1.4 %pack_ids.1 = s32[128,128]{1,0:T(8,128)} custom-call(s32[16,128]{1,0:T(8,128)} %bitcast.11, s32[8,128]{1,0:T(8,128)} %bitcast.12, s32[1,128]{1,0:T(1,128)} %req_count_ref.1, s32[1,128]{1,0:T(1,128)} %halo_count_ref.1), custom_call_target="tpu_custom_call" | custom-call | tf_op jit(solution)/shard_map/pack_ids/pallas_call | solution.py:33
  1.4 11.5 %all-to-all-start = ((s32[128,1,128]{2,1,0:T(1,128)}), s32[128,1,128]{2,1,0:T(1,128)S(1)}, u32[]{:S(2)}, u32[]{:S(2)}) async-start(s32[128,1,128]{2,1,0:T(1,128)} %bitcast.5), calls=%async_computation | async-start | bytes 131072 | tf_op jit(solution)/shard_map/all_to_all | solution.py:362
  13.0 2.7 %project.1 = (bf16[1024,256]{1,0:T(8,128)(2,1)S(1)}, bf16[1024,256]{1,0:T(8,128)(2,1)S(1)}) custom-call(f32[1024,768]{1,0:T(8,128)} %features_ref.1, f32[1024,256]{1,0:T(8,128)} %history_ref.1, bf16[768,256]{1,0:T(8,128)(2,1)} %w_in_ref.1), custom_call_target="tpu_custom_call" | custom-call | flops 402653184 | bytes 5242880 | tf_op jit(solution)/shard_map/project/pallas_call | solution.py:80
  15.7 6.8 %all-to-all-done = s32[128,1,128]{2,1,0:T(1,128)S(1)} async-done(((s32[128,1,128]{2,1,0:T(1,128)}), s32[128,1,128]{2,1,0:T(1,128)S(1)}, u32[]{:S(2)}, u32[]{:S(2)}) %all-to-all-start) | async-done | bytes 65568 | tf_op jit(solution)/shard_map/all_to_all | solution.py:362
  22.5 2.7 %pick_rows.1 = bf16[128,24,256]{2,1,0:T(8,128)(2,1)} custom-call(s32[128,128]{1,0:T(8,128)S(1)} %bitcast.10, bf16[1024,256]{1,0:T(8,128)(2,1)S(1)} %get-tuple-element.11.proj_ref, bf16[1024,256]{1,0:T(8,128)(2,1)S(1)} %get-tuple-element.12.hist_ref), custom_call_target="tpu_custom_call" | custom-call | flops 1610612736 | bytes 3145728 | tf_op jit(solution)/shard_map/pick_rows/pallas_call | solution.py:149
  25.2 4.5 %all-to-all-start.1 = ((bf16[128,24,256]{2,1,0:T(8,128)(2,1)}), bf16[128,24,256]{2,1,0:T(8,128)(2,1)S(1)}, u32[]{:S(2)}, u32[]{:S(2)}) async-start(bf16[128,24,256]{2,1,0:T(8,128)(2,1)} %pick_rows.1), calls=%async_computation.1 | async-start | bytes 3145728 | tf_op jit(solution)/shard_map/all_to_all | solution.py:366
  30.4 0.0 copy-start
  30.4 11.2 %build_dense.1 = (bf16[256,3072]{1,0:T(8,128)(2,1)S(1)}, bf16[1792,3072]{1,0:T(8,128)(2,1)}) custom-call(s32[512]{0:T(512)} %rows_ref.1, s32[512]{0:T(512)} %cols_ref.1, s32[1]{0:T(128)S(6)} %copy.14.used_ref, bf16[512,128,128]{2,1,0:T(8,128)(2,1)} %tiles_ref.1), custom_call_target="tpu_custom_call" | custom-call | flops 1048576 | bytes 31457280 | tf_op jit(solution)/shard_map/build_dense/pallas_call | solution.py:237
  41.6 13.1 %all-to-all-done.1.came_ref = bf16[128,24,256]{2,1,0:T(8,128)(2,1)S(1)} async-done(((bf16[128,24,256]{2,1,0:T(8,128)(2,1)}), bf16[128,24,256]{2,1,0:T(8,128)(2,1)S(1)}, u32[]{:S(2)}, u32[]{:S(2)}) %all-to-all-start.1) | async-done | bytes 1572896 | tf_op jit(solution)/shard_map/all_to_all | solution.py:366
  54.7 0.0 copy-done
  54.7 6.1 %combine.1 = bf16[2048,256]{1,0:T(8,128)(2,1)} custom-call(bf16[256,3072]{1,0:T(8,128)(2,1)S(1)} %get-tuple-element.14.kept_ref, bf16[1792,3072]{1,0:T(8,128)(2,1)} %get-tuple-element.15.dense_ref, bf16[128,24,256]{2,1,0:T(8,128)(2,1)S(1)} %all-to-all-done.1.came_ref, bf16[256,256]{1,0:T(8,128)(2,1)S(1)} %copy-done), custom_call_target="tpu_custom_call" | custom-call | flops 3221225472 | bytes 16777216 | tf_op jit(solution)/shard_map/combine/pallas_call | solution.py:323
Async XLA Ops:
  1.4 21.0 %all-to-all-start = ((s32[128,1,128]{2,1,0:T(1,128)}), s32[128,1,128]{2,1,0:T(1,128)S(1)}, u32[]{:S(2)}, u32[]{:S(2)}) async-start(s32[128,1,128]{2,1,0:T(1,128)} %bitcast.5), calls=%async_computation | async-start | bytes 131072 | tf_op jit(solution)/shard_map/all_to_all | solution.py:362
  25.2 29.4 %all-to-all-start.1 = ((bf16[128,24,256]{2,1,0:T(8,128)(2,1)}), bf16[128,24,256]{2,1,0:T(8,128)(2,1)S(1)}, u32[]{:S(2)}, u32[]{:S(2)}) async-start(bf16[128,24,256]{2,1,0:T(8,128)(2,1)} %pick_rows.1), calls=%async_computation.1 | async-start | bytes 3145728 | tf_op jit(solution)/shard_map/all_to_all | solution.py:366
  30.4 24.3 %copy-start = (bf16[256,256]{1,0:T(8,128)(2,1)S(1)}, bf16[256,256]{1,0:T(8,128)(2,1)}, u32[]{:S(2)}) copy-start(bf16[256,256]{1,0:T(8,128)(2,1)} %w_ref.1) | copy-start | bytes 393220
